TPU v7x, 32 devices: a whole 2x2x4 slice. The times are simulated.
32 devices in a mesh: dp: 16 (over z, x, core), mp: 2 (over y).
Axes of the slice: x: 2, y: 2, z: 4, core: 2. Of those that a mesh axis runs over, the one named last changes fastest.
Arguments:
- tokens: bfloat16 [64, 256, 1152], P('dp'), may hold values from -6 to 6
- conditioning: bfloat16 [64, 1152], P('dp'), may hold values from -6 to 6
- bucket_ids: int32 [64], P('dp'), may hold values from 0 to 2, as said below
- keep_order: int32 [64, 128], P('dp'), may hold values from 0 to 255, as said below
- group_counts: int32 [16], P('dp'), may hold values from 1 to 4, as said below
- cotangent: bfloat16 [64, 256, 1152], P('dp'), may hold values from -6 to 6
- modulation_weight: bfloat16 [1152, 6912], P('dp'), may hold values from -0.1875 to 0.1875
- modulation_bias: bfloat16 [6912], replicated, may hold values from -3 to 3
- input_weight: bfloat16 [3, 1152, 1152], P(None, 'dp', 'mp'), may hold values from -0.1875 to 0.1875
- query_value_bias: bfloat16 [2, 1152], P(None, 'mp'), may hold values from -3 to 3
- output_weight: bfloat16 [1152, 1152], P('mp', 'dp'), may hold values from -0.75 to 0.75
- output_bias: bfloat16 [1152], replicated, may hold values from -2 to 2
- expand_weight: bfloat16 [1152, 4608], P('dp', 'mp'), may hold values from -0.1875 to 0.1875
- expand_bias: bfloat16 [4608], P('mp'), may hold values from -3 to 3
- shrink_weight: bfloat16 [4608, 1152], P('mp', 'dp'), may hold values from -0.09375 to 0.09375
- shrink_bias: bfloat16 [1152], replicated, may hold values from -2 to 2
Outputs:
- block_out: bfloat16 [64, 256, 1152], P('dp')
- tokens_grad: bfloat16 [64, 256, 1152], P('dp')
- modulation_weight_grad: float32 [1152, 6912], P('dp')
- modulation_bias_grad: float32 [6912], replicated
- input_weight_grad: float32 [3, 1152, 1152], P(None, 'dp', 'mp')
- query_value_bias_grad: float32 [2, 1152], P(None, 'mp')
- output_weight_grad: float32 [1152, 1152], P('mp', 'dp')
- output_bias_grad: float32 [1152], replicated
- expand_weight_grad: float32 [1152, 4608], P('dp', 'mp')
- expand_bias_grad: float32 [4608], P('mp')
- shrink_weight_grad: float32 [4608, 1152], P('mp', 'dp')
- shrink_bias_grad: float32 [1152], replicated
Inputs may be any that keep to these rules, and one draw needn't show every extreme that they name: `bucket_ids`: buckets 0, 1 and 2 stand for grids of 16 x 16, 12 x 20 and 20 x 12 patches. `keep_order`: row i holds 128 distinct slot numbers; its first valid-length entries (half of image i's length) are real token slots of that image chosen at random, the remaining entries are other slots of that image. Group g holds live images in its first group_counts[g] of 4 image slots; in every draw some group is full.
All inputs are finite; a program needn't handle non-finite values.
Results may differ from a plain program's by a relative error of at most 0.015.
The roundings to bfloat16 on the way count: a program that leaves them out, or rounds other values in their place, can miss the bound.
Values may be sent and summed in bfloat16 or wider, within the bound.
A program may use at most 144 MiB of HBM per device.

v0:
```python
import jax
import jax.numpy as jnp
from jax import lax
from jax.sharding import PartitionSpec as P

HEAD_DIM = 72
MICRO = 2


EPSILON = 1e-06


def normalize(rows):
    center = rows - jnp.mean(rows, axis=-1, keepdims=True)
    spread = jnp.mean(center * center, axis=-1, keepdims=True)
    return center * lax.rsqrt(spread + EPSILON)


def modulated(rows, shift, scale):
    return normalize(rows) * (1.0 + scale) + shift


def gelu_tanh(values):
    return jax.nn.gelu(values, approximate=True)


def model_total_sum(partial_value):
    share = lax.psum_scatter(partial_value, "mp", scatter_dimension=2, tiled=True)
    return lax.all_gather(share, "mp", axis=2, tiled=True)


def gather_weights(modulation_weight, input_weight, output_weight, expand_weight, shrink_weight):
    return (
        lax.all_gather(modulation_weight, "dp", axis=0, tiled=True),
        lax.all_gather(input_weight, "dp", axis=1, tiled=True),
        lax.all_gather(output_weight, "dp", axis=1, tiled=True),
        lax.all_gather(expand_weight, "dp", axis=0, tiled=True),
        lax.all_gather(shrink_weight, "dp", axis=1, tiled=True),
    )


def scatter_every(terms):
    return (
        lax.psum_scatter(terms[0], "dp", scatter_dimension=0, tiled=True),
        lax.psum_scatter(terms[1], "dp", scatter_dimension=1, tiled=True),
        lax.psum_scatter(terms[2], "dp", scatter_dimension=1, tiled=True),
        lax.psum_scatter(terms[3], "dp", scatter_dimension=0, tiled=True),
        lax.psum_scatter(terms[4], "dp", scatter_dimension=1, tiled=True),
    )


def attention_scores(query, key_rows, keymask, scale_factor):
    scores = (
        jnp.einsum("bqhd,bkhd->bhqk", query, key_rows, preferred_element_type=jnp.float32)
        * scale_factor
    )
    return jnp.where(keymask[:, None, None, :], scores, -1e30)


def run_micro(tokens_mb, cond_mb, order_mb, valid_mb, grad_mb, full, biases):
    mod_w, incoming_weight, outgoing_weight, expert_weight_rows, narrowing_weight = full
    mod_bias, qv_bias, outgoing_bias, expert_bias_rows, narrowing_bias = biases
    batch, keep = order_mb.shape
    width = tokens_mb.shape[2]
    inner = incoming_weight.shape[2]
    heads_here = inner // HEAD_DIM
    scale_factor = HEAD_DIM ** (-0.5)
    single_float32 = jnp.float32
    bf16 = jnp.bfloat16
    batch_rows = jnp.arange(batch)[:, None]
    keymask = jnp.arange(keep)[None, :] < valid_mb[:, None]
    rowmask = keymask[:, :, None]
    hidden_in = jnp.take_along_axis(tokens_mb, order_mb[:, :, None], axis=1).astype(single_float32)
    silu_cond = jax.nn.silu(cond_mb.astype(single_float32)).astype(bf16)
    modulation = jnp.dot(silu_cond, mod_w, preferred_element_type=single_float32) + mod_bias
    pieces = modulation.reshape(batch, 6, 1, width)
    shift_one, scale_one, gate_one = (pieces[:, 0], pieces[:, 1], pieces[:, 2])
    shift_two, scale_two, gate_two = (pieces[:, 3], pieces[:, 4], pieces[:, 5])
    first, pull_first = jax.vjp(modulated, hidden_in, shift_one, scale_one)
    first_reduced = first.astype(bf16)
    projected_rows = jnp.einsum(
        "mzu,lug->lmzg", first_reduced, incoming_weight, preferred_element_type=single_float32
    )
    query = (projected_rows[0] + qv_bias[0]).astype(bf16).reshape(batch, keep, heads_here, HEAD_DIM)
    key_rows = projected_rows[1].astype(bf16).reshape(batch, keep, heads_here, HEAD_DIM)
    value = (projected_rows[2] + qv_bias[1]).astype(bf16).reshape(batch, keep, heads_here, HEAD_DIM)
    scores = attention_scores(query, key_rows, keymask, scale_factor)
    top = jnp.max(scores, axis=-1, keepdims=True)
    expo = jnp.exp(scores - top)
    total = jnp.sum(expo, axis=-1, keepdims=True)
    probs = expo / total
    log_total = top + jnp.log(total)
    attention_result = (
        jnp.einsum(
            "bhqk,bkhd->bqhd", probs.astype(bf16), value, preferred_element_type=single_float32
        )
        .astype(bf16)
        .reshape(batch, keep, inner)
    )
    attn_out = (
        model_total_sum(
            jnp.einsum(
                "hfc,cj->hfj",
                attention_result,
                outgoing_weight,
                preferred_element_type=single_float32,
            )
        )
        + outgoing_bias
    )
    middle = hidden_in + gate_one * attn_out
    second, pull_second = jax.vjp(modulated, middle, shift_two, scale_two)
    second_reduced = second.astype(bf16)
    preactivation_rows = (
        jnp.einsum(
            "get,tm->gem", second_reduced, expert_weight_rows, preferred_element_type=single_float32
        )
        + expert_bias_rows
    )
    activated, pull_act = jax.vjp(gelu_tanh, preactivation_rows)
    activation_reduced = activated.astype(bf16)
    mlp_out = (
        model_total_sum(
            jnp.einsum(
                "xwl,lc->xwc",
                activation_reduced,
                narrowing_weight,
                preferred_element_type=single_float32,
            )
        )
        + narrowing_bias
    )
    routed_out = jnp.where(rowmask, middle + gate_two * mlp_out, hidden_in)
    block_mb = tokens_mb.at[batch_rows, order_mb].set(routed_out.astype(bf16))
    grad_rows = jnp.take_along_axis(grad_mb, order_mb[:, :, None], axis=1).astype(single_float32)
    grad_final = jnp.where(rowmask, grad_rows, 0.0)
    grad_skip = grad_rows - grad_final
    grad_gate_two = jnp.sum(mlp_out * grad_final, axis=1, keepdims=True)
    grad_mlp = gate_two * grad_final
    perceptron_gradient_reduced = grad_mlp.astype(bf16)
    narrowing_term = jnp.einsum(
        "ehm,eht->mt",
        activation_reduced,
        perceptron_gradient_reduced,
        preferred_element_type=single_float32,
    )
    (grad_pre,) = pull_act(
        jnp.einsum(
            "awm,hm->awh",
            perceptron_gradient_reduced,
            narrowing_weight,
            preferred_element_type=single_float32,
        )
    )
    preactivation_gradient_reduced = grad_pre.astype(bf16)
    widening_term = jnp.einsum(
        "cnq,cne->qe",
        second_reduced,
        preactivation_gradient_reduced,
        preferred_element_type=single_float32,
    )
    grad_second = model_total_sum(
        jnp.einsum(
            "pem,sm->pes",
            preactivation_gradient_reduced,
            expert_weight_rows,
            preferred_element_type=single_float32,
        )
    )
    grad_middle, grad_shift_two, grad_scale_two = pull_second(grad_second)
    grad_middle = grad_middle + grad_final
    grad_gate_one = jnp.sum(attn_out * grad_middle, axis=1, keepdims=True)
    grad_attn = gate_one * grad_middle
    attention_gradient_reduced = grad_attn.astype(bf16)
    output_summand = jnp.einsum(
        "tyo,tyq->oq",
        attention_result,
        attention_gradient_reduced,
        preferred_element_type=single_float32,
    )
    grad_attended = (
        jnp.einsum(
            "znx,ox->zno",
            attention_gradient_reduced,
            outgoing_weight,
            preferred_element_type=single_float32,
        )
        .astype(bf16)
        .reshape(batch, keep, heads_here, HEAD_DIM)
    )
    again = attention_scores(query, key_rows, keymask, scale_factor)
    probs_again = jnp.exp(again - log_total)
    grad_probs = jnp.einsum(
        "bqhd,bkhd->bhqk", grad_attended, value, preferred_element_type=single_float32
    )
    grad_value = jnp.einsum(
        "bhqk,bqhd->bkhd",
        probs_again.astype(bf16),
        grad_attended,
        preferred_element_type=single_float32,
    )
    inner_sum = jnp.sum(probs_again * grad_probs, axis=-1, keepdims=True)
    grad_scores = (probs_again * (grad_probs - inner_sum)).astype(bf16)
    grad_query = (
        jnp.einsum("bhqk,bkhd->bqhd", grad_scores, key_rows, preferred_element_type=single_float32)
        * scale_factor
    )
    grad_key = (
        jnp.einsum("bhqk,bqhd->bkhd", grad_scores, query, preferred_element_type=single_float32)
        * scale_factor
    )
    grad_proj = jnp.stack([grad_query, grad_key, grad_value]).reshape(3, batch, keep, inner)
    query_value_term = jnp.sum(grad_proj[::2], axis=(1, 2))
    projection_gradient_reduced = grad_proj.astype(bf16)
    input_summand = jnp.einsum(
        "iyj,fiyu->fju",
        first_reduced,
        projection_gradient_reduced,
        preferred_element_type=single_float32,
    )
    grad_first = model_total_sum(
        jnp.einsum(
            "pniu,psu->nis",
            projection_gradient_reduced,
            incoming_weight,
            preferred_element_type=single_float32,
        )
    )
    grad_hidden, grad_shift_one, grad_scale_one = pull_first(grad_first)
    grad_total = grad_hidden + grad_middle + grad_skip
    tokens_mb_grad = grad_mb.at[batch_rows, order_mb].set(grad_total.astype(bf16))
    grad_mod = jnp.concatenate(
        [
            grad_shift_one,
            grad_scale_one,
            grad_gate_one,
            grad_shift_two,
            grad_scale_two,
            grad_gate_two,
        ],
        axis=1,
    ).reshape(batch, 6 * width)
    terms = (input_summand, output_summand, widening_term, narrowing_term)
    bias_terms = (
        jnp.sum(grad_mod, axis=0),
        query_value_term,
        jnp.sum(grad_attn, axis=(0, 1)),
        jnp.sum(grad_pre, axis=(0, 1)),
        jnp.sum(grad_mlp, axis=(0, 1)),
    )
    return (block_mb, tokens_mb_grad, terms, bias_terms, silu_cond, grad_mod.astype(bf16))


def body(
    tokens,
    conditioning,
    bucket_ids,
    keep_order,
    group_counts,
    cotangent,
    modulation_weight,
    modulation_bias,
    input_weight,
    query_value_bias,
    output_weight,
    output_bias,
    expand_weight,
    expand_bias,
    shrink_weight,
    shrink_bias,
):
    local = tokens.shape[0]
    per_micro = local // MICRO
    slots = tokens.shape[1]
    lengths = jnp.where(bucket_ids == 0, slots, slots - slots // 16) // 2
    valid = jnp.where(jnp.arange(local) < group_counts[0], lengths, 0).astype(jnp.int32)
    biases = (
        modulation_bias.astype(jnp.float32),
        query_value_bias.astype(jnp.float32),
        output_bias.astype(jnp.float32),
        expand_bias.astype(jnp.float32),
        shrink_bias.astype(jnp.float32),
    )
    block_parts = []
    grad_parts = []
    weight_sums = None
    bias_sums = None
    for micro in range(MICRO):
        full = gather_weights(
            modulation_weight, input_weight, output_weight, expand_weight, shrink_weight
        )
        begin = micro * per_micro
        finish = begin + per_micro
        block_mb, grad_mb, terms, bias_terms, silu_cond, grad_mod_low = run_micro(
            tokens[begin:finish],
            conditioning[begin:finish],
            keep_order[begin:finish],
            valid[begin:finish],
            cotangent[begin:finish],
            full,
            biases,
        )
        block_parts.append(block_mb)
        grad_parts.append(grad_mb)
        mod_term = jnp.einsum(
            "bd,be->de", silu_cond, grad_mod_low, preferred_element_type=jnp.float32
        )
        terms = (mod_term,) + tuple(terms)
        terms = scatter_every(terms)
        if weight_sums is None:
            weight_sums = tuple(terms)
            bias_sums = bias_terms
        else:
            weight_sums = tuple((left + right for left, right in zip(weight_sums, terms)))
            bias_sums = tuple((left + right for left, right in zip(bias_sums, bias_terms)))
    bias_sums = lax.psum(
        (bias_sums[0], bias_sums[1], bias_sums[2], bias_sums[3], bias_sums[4]), "dp"
    )
    return (
        jnp.concatenate(block_parts, axis=0),
        jnp.concatenate(grad_parts, axis=0),
        weight_sums[0],
        bias_sums[0],
        weight_sums[1],
        bias_sums[1],
        weight_sums[2],
        bias_sums[2],
        weight_sums[3],
        bias_sums[3],
        weight_sums[4],
        bias_sums[4],
    )


def solution(mesh):
    in_specs = (
        P("dp", None, None),
        P("dp", None),
        P("dp"),
        P("dp", None),
        P("dp"),
        P("dp", None, None),
        P("dp", None),
        P(),
        P(None, "dp", "mp"),
        P(None, "mp"),
        P("mp", "dp"),
        P(),
        P("dp", "mp"),
        P("mp"),
        P("mp", "dp"),
        P(),
    )
    out_specs = (
        P("dp", None, None),
        P("dp", None, None),
        P("dp", None),
        P(),
        P(None, "dp", "mp"),
        P(None, "mp"),
        P("mp", "dp"),
        P(),
        P("dp", "mp"),
        P("mp"),
        P("mp", "dp"),
        P(),
    )
    return jax.shard_map(body, mesh=mesh, in_specs=in_specs, out_specs=out_specs, check_vma=False)
```

profile of v0, /device:TPU:0, one launch (start us, length us, event | category | flops | bytes accessed | tf_op | source)
XLA Modules:
  0.0 1632.5 jit_solution(14965664791636846735)
XLA Ops:
  18.7 115.8 %all-gather.14.cloned.1.call-done = bf16[1152,6912]{1,0:T(8,128)(2,1)} async-done(((bf16[72,6912]{1,0:T(8,128)(2,1)}), bf16[1152,6912]{1,0:T(8,128)(2,1)}) %all-gather.14.cloned.1.call-update) | async-done | bytes 15925264 | tf_op jit(solution)/shard_map/all_gather | solution.py:34
  142.3 44.3 %all-gather.16.cloned.1.call-done = bf16[3,1152,576]{2,1,0:T(8,128)(2,1)} async-done(((bf16[3,72,576]{2,1,0:T(8,128)(2,1)}), bf16[3,1152,576]{2,1,0:T(8,128)(2,1)}) %all-gather.16.cloned.1.call-update) | async-done | bytes 3981328 | tf_op jit(solution)/shard_map/all_gather | solution.py:35
  193.7 33.0 %all-gather.18.cloned.1.call-done = bf16[576,1152]{0,1:T(8,128)(2,1)} async-done(((bf16[576,72]{0,1:T(8,128)(2,1)}), bf16[576,1152]{0,1:T(8,128)(2,1)}) %all-gather.18.cloned.1.call-update) | async-done | bytes 1327120 | tf_op jit(solution)/shard_map/all_gather | solution.py:36
  229.8 20.7 %reduce-scatter.15.cloned.1.call-done = f32[2,128,576]{1,2,0:T(8,128)} async-done(((f32[2,128,1152]{1,2,0:T(8,128)}), f32[2,128,576]{1,2,0:T(8,128)}) %reduce-scatter.15.cloned.1.call-update) | async-done | bytes 589840 | tf_op jit(solution)/shard_map/reduce_scatter | solution.py:28
  278.5 54.9 %all-gather.22.cloned.1.call-done = bf16[1152,2304]{1,0:T(8,128)(2,1)} async-done(((bf16[72,2304]{1,0:T(8,128)(2,1)}), bf16[1152,2304]{1,0:T(8,128)(2,1)}) %all-gather.22.cloned.1.call-update) | async-done | bytes 5308432 | tf_op jit(solution)/shard_map/all_gather | solution.py:37
  339.2 51.5 %all-gather.24.cloned.1.call-done = bf16[2304,1152]{0,1:T(8,128)(2,1)} async-done(((bf16[2304,72]{0,1:T(8,128)(2,1)}), bf16[2304,1152]{0,1:T(8,128)(2,1)}) %all-gather.24.cloned.1.call-update) | async-done | bytes 5308432 | tf_op jit(solution)/shard_map/all_gather | solution.py:38
  431.2 15.5 reduce-scatter.19.cloned.1.call-done
  447.6 23.4 %all-gather.32.cloned.1.call-done = f32[2,128,1152]{1,2,0:T(8,128)} async-done(((f32[2,128,576]{1,2,0:T(8,128)}), f32[2,128,1152]{1,2,0:T(8,128)}) %all-gather.32.cloned.1.call-update) | async-done | bytes 1179664 | tf_op jit(solution)/shard_map/all_gather | solution.py:29
  475.0 20.4 %all-gather.28.cloned.1.call-done = f32[2,128,1152]{1,2,0:T(8,128)} async-done(((f32[2,128,576]{1,2,0:T(8,128)}), f32[2,128,1152]{1,2,0:T(8,128)}) %all-gather.28.cloned.1.call-update) | async-done | bytes 1179664 | tf_op jit(solution)/shard_map/all_gather | solution.py:29
  517.3 21.9 %reduce-scatter.27.cloned.1.call-done = f32[2,128,576]{1,2,0:T(8,128)} async-done(((f32[2,128,1152]{1,2,0:T(8,128)}), f32[2,128,576]{1,2,0:T(8,128)}) %reduce-scatter.27.cloned.1.call-update) | async-done | bytes 589840 | tf_op jit(solution)/shard_map/reduce_scatter | solution.py:28
  587.5 23.9 %reduce-scatter.25.cloned.1.call-done = f32[2,128,576]{1,2,0:T(8,128)} async-done(((f32[2,128,1152]{1,2,0:T(8,128)}), f32[2,128,576]{1,2,0:T(8,128)}) %reduce-scatter.25.cloned.1.call-update) | async-done | bytes 589840 | tf_op jit(solution)/shard_map/reduce_scatter | solution.py:28
  611.4 24.4 %reduce-scatter.21.cloned.1.call-done = f32[2,128,576]{1,2,0:T(8,128)} async-done(((f32[2,128,1152]{1,2,0:T(8,128)}), f32[2,128,576]{1,2,0:T(8,128)}) %reduce-scatter.21.cloned.1.call-update) | async-done | bytes 589840 | tf_op jit(solution)/shard_map/reduce_scatter | solution.py:28
  635.9 23.9 %reduce-scatter.29.cloned.1.call-done = f32[2,128,576]{1,2,0:T(8,128)} async-done(((f32[2,128,1152]{1,2,0:T(8,128)}), f32[2,128,576]{1,2,0:T(8,128)}) %reduce-scatter.29.cloned.1.call-update) | async-done | bytes 589840 | tf_op jit(solution)/shard_map/reduce_scatter | solution.py:28
  732.5 24.4 %all-gather.38.cloned.1.call-done = f32[2,128,1152]{1,2,0:T(8,128)} async-done(((f32[2,128,576]{1,2,0:T(8,128)}), f32[2,128,1152]{1,2,0:T(8,128)}) %all-gather.38.cloned.1.call-update) | async-done | bytes 1179664 | tf_op jit(solution)/shard_map/all_gather | solution.py:29
  763.7 25.0 %convolution_add_fusion = f32[1152,6912]{1,0:T(8,128)} fusion(f32[1152,6912]{1,0:T(8,128)} %fusion.178, bf16[2,6912]{1,0:T(2,128)(2,1)S(1)} %bitcast.353, bf16[4,1152]{1,0:T(4,128)(2,1)S(1)} %copy-done.78), kind=kOutput, calls=%fused_computation.8 | convolution fusion | flops 39826944 | bytes 63733248 | tf_op jit(solution)/shard_map/bd,be->de/dot_general | solution.py:305
  798.2 17.7 %scatter_fusion.2 = bf16[2,256,1152]{2,1,0:T(8,128)(2,1)S(1)} fusion(bf16[2,256,1152]{2,1,0:T(8,128)(2,1)S(1)} %copy-done.7, s32[256]{0:T(256)S(1)} %copy-done.10, bf16[256,1152]{1,0:T(8,128)(2,1)S(1)} %bitcast.322), kind=kCustom, calls=%fused_computation.6 | custom fusion | bytes 1771520 | tf_op jit(solution)/shard_map/scatter | solution.py:231
  816.0 26.9 %scatter_fusion = bf16[2,256,1152]{2,1,0:T(8,128)(2,1)S(1)} fusion(bf16[2,256,1152]{2,1,0:T(8,128)(2,1)S(1)} %copy-done.3, s32[256]{0:T(256)S(1)} %copy-done.10, bf16[256,1152]{1,0:T(8,128)(2,1)} %bitcast.321), kind=kCustom, calls=%fused_computation.4 | custom fusion | bytes 1771520 | tf_op jit(solution)/shard_map/scatter | solution.py:134
  852.4 26.6 %scatter_fusion.3 = bf16[2,256,1152]{2,1,0:T(8,128)(2,1)S(1)} fusion(bf16[2,256,1152]{2,1,0:T(8,128)(2,1)S(1)} %copy-done.5, s32[256]{0:T(256)S(1)} %copy-done.9, bf16[256,1152]{1,0:T(8,128)(2,1)} %bitcast.319), kind=kCustom, calls=%fused_computation.7 | custom fusion | bytes 1771520 | tf_op jit(solution)/shard_map/scatter | solution.py:231
  879.0 26.6 %scatter_fusion.1 = bf16[2,256,1152]{2,1,0:T(8,128)(2,1)S(1)} fusion(bf16[2,256,1152]{2,1,0:T(8,128)(2,1)S(1)} %copy-done.1, s32[256]{0:T(256)S(1)} %copy-done.9, bf16[256,1152]{1,0:T(8,128)(2,1)} %bitcast.320), kind=kCustom, calls=%fused_computation.5 | custom fusion | bytes 1771520 | tf_op jit(solution)/shard_map/scatter | solution.py:134
  907.0 63.8 %all-reduce.2 = (f32[6912]{0:T(1024)}, f32[2,576]{1,0:T(2,128)}, f32[1152]{0:T(1024)}, f32[2304]{0:T(1024)}, f32[1152]{0:T(1024)}) all-reduce(f32[6912]{0:T(1024)} %add.447, f32[2,576]{1,0:T(2,128)} %add.449, f32[1152]{0:T(1024)} %add.451, f32[2304]{0:T(1024)S(1)} %copy-done.118, f32[1152]{0:T(1024)} %add.455), channel_id=1, replica_groups=mesh['dp'=16,'mp'=2] {'dp'}, use_global_device_ids=true, to_apply=%region_50.52 | all-reduce | flops 12672 | bytes 101376 | tf_op jit(solution)/shard_map/psum | solution.py:316
  984.2 67.8 %reduce-scatter.37.cloned.1.call-done = f32[576,72]{0,1:T(8,128)} async-done(((f32[576,1152]{0,1:T(8,128)}), f32[576,72]{0,1:T(8,128)}) %reduce-scatter.37.cloned.1.call-update) | async-done | bytes 165904
  1052.0 123.8 %reduce-scatter.35.cloned.1.call-done = f32[2304,72]{0,1:T(8,128)} async-done(((f32[2304,1152]{0,1:T(8,128)}), f32[2304,72]{0,1:T(8,128)}) %reduce-scatter.35.cloned.1.call-update) | async-done | bytes 663568 | tf_op jit(solution)/shard_map/reduce_scatter | solution.py:48
  1175.8 124.7 %reduce-scatter.33.cloned.1.call-done = f32[72,2304]{1,0:T(8,128)} async-done(((f32[1152,2304]{1,0:T(8,128)}), f32[72,2304]{1,0:T(8,128)}) %reduce-scatter.33.cloned.1.call-update) | async-done | bytes 663568 | tf_op jit(solution)/shard_map/reduce_scatter | solution.py:47
  1300.5 325.0 %reduce-scatter.31.cloned.1.call-done = f32[72,6912]{1,0:T(8,128)} async-done(((f32[1152,6912]{1,0:T(8,128)}), f32[72,6912]{1,0:T(8,128)}) %reduce-scatter.31.cloned.1.call-update) | async-done | bytes 1990672 | tf_op jit(solution)/shard_map/reduce_scatter | solution.py:44
  (589 shorter events, 288.7 us)
Async XLA Ops:
  7.2 127.3 %all-gather.14.cloned.1.call-start = ((), (), s32[]{:S(2)}) async-start(), calls=%async_computation.12 | async-start | bytes 16920576 | tf_op jit(solution)/shard_map/all_gather | solution.py:34
  8.0 178.7 %all-gather.16.cloned.1.call-start = ((), (), s32[]{:S(2)}) async-start(), calls=%async_computation.13 | async-start | bytes 4700160 | tf_op jit(solution)/shard_map/all_gather | solution.py:35
  8.7 218.0 %all-gather.18.cloned.1.call-start = ((), (), s32[]{:S(2)}) async-start(), calls=%async_computation.14 | async-start | bytes 1566720 | tf_op jit(solution)/shard_map/all_gather | solution.py:36
  9.4 241.0 %reduce-scatter.15.cloned.1.call-start = ((), (), s32[]{:S(2)}) async-start(), calls=%async_computation.15 | async-start | bytes 1769472 | tf_op jit(solution)/shard_map/reduce_scatter | solution.py:28
  250.5 82.9 %all-gather.22.cloned.1.call-start = ((), (), s32[]{:S(2)}) async-start(), calls=%async_computation.17 | async-start | bytes 5640192 | tf_op jit(solution)/shard_map/all_gather | solution.py:37
  251.0 139.7 %all-gather.24.cloned.1.call-start = ((), (), s32[]{:S(2)}) async-start(), calls=%async_computation.18 | async-start | bytes 5640192 | tf_op jit(solution)/shard_map/all_gather | solution.py:38
  251.8 171.6 %reduce-scatter.23.cloned.1.call-start = ((), (), s32[]{:S(2)}) async-start(), calls=%async_computation.25 | async-start | bytes 1769472 | tf_op jit(solution)/shard_map/reduce_scatter | solution.py:28
  423.3 47.6 %all-gather.32.cloned.1.call-start = ((), (), s32[]{:S(2)}) async-start(), calls=%async_computation.26 | async-start | bytes 1769472 | tf_op jit(solution)/shard_map/all_gather | solution.py:29
  423.9 71.5 %all-gather.28.cloned.1.call-start = ((), (), s32[]{:S(2)}) async-start(), calls=%async_computation.22 | async-start | bytes 1769472 | tf_op jit(solution)/shard_map/all_gather | solution.py:29
  446.7 92.5 %reduce-scatter.27.cloned.1.call-start = ((), (), s32[]{:S(2)}) async-start(), calls=%async_computation.29 | async-start | bytes 1769472 | tf_op jit(solution)/shard_map/reduce_scatter | solution.py:28
  517.2 48.8 %all-gather.36.cloned.1.call-start = ((), (), s32[]{:S(2)}) async-start(), calls=%async_computation.30 | async-start | bytes 1769472 | tf_op jit(solution)/shard_map/all_gather | solution.py:29
  539.2 48.2 %reduce-scatter.17.cloned.1.call-start = ((), (), s32[]{:S(2)}) async-start(), calls=%async_computation.19 | async-start | bytes 1769472 | tf_op jit(solution)/shard_map/reduce_scatter | solution.py:28
  545.2 66.2 %reduce-scatter.25.cloned.1.call-start = ((), (), s32[]{:S(2)}) async-start(), calls=%async_computation.27 | async-start | bytes 1769472 | tf_op jit(solution)/shard_map/reduce_scatter | solution.py:28
  558.6 77.2 %reduce-scatter.21.cloned.1.call-start = ((), (), s32[]{:S(2)}) async-start(), calls=%async_computation.23 | async-start | bytes 1769472 | tf_op jit(solution)/shard_map/reduce_scatter | solution.py:28
  566.0 93.8 %reduce-scatter.29.cloned.1.call-start = ((), (), s32[]{:S(2)}) async-start(), calls=%async_computation.31 | async-start | bytes 1769472 | tf_op jit(solution)/shard_map/reduce_scatter | solution.py:28
  584.3 122.7 %all-gather.26.cloned.1.call-start = ((), (), s32[]{:S(2)}) async-start(), calls=%async_computation.20 | async-start | bytes 1769472 | tf_op jit(solution)/shard_map/all_gather | solution.py:29
  587.4 120.9 %all-gather.34.cloned.1.call-start = ((), (), s32[]{:S(2)}) async-start(), calls=%async_computation.28 | async-start | bytes 1769472 | tf_op jit(solution)/shard_map/all_gather | solution.py:29
  611.4 121.2 %all-gather.30.cloned.1.call-start = ((), (), s32[]{:S(2)}) async-start(), calls=%async_computation.24 | async-start | bytes 1769472 | tf_op jit(solution)/shard_map/all_gather | solution.py:29
  635.8 121.1 %all-gather.38.cloned.1.call-start = ((), (), s32[]{:S(2)}) async-start(), calls=%async_computation.32 | async-start | bytes 1769472 | tf_op jit(solution)/shard_map/all_gather | solution.py:29
  659.8 322.3 %all-reduce.5.cloned.1.call-start = ((), (), s32[]{:S(2)}) async-start(), calls=%async_computation.36 | async-start | bytes 23592960
  681.7 370.3 %reduce-scatter.37.cloned.1.call-start = ((), (), s32[]{:S(2)}) async-start(), calls=%async_computation.37 | async-start | bytes 3133440
  686.6 489.2 %reduce-scatter.35.cloned.1.call-start = ((), (), s32[]{:S(2)}) async-start(), calls=%async_computation.35 | async-start | bytes 11280384 | tf_op jit(solution)/shard_map/reduce_scatter | solution.py:48
  696.0 604.5 %reduce-scatter.33.cloned.1.call-start = ((), (), s32[]{:S(2)}) async-start(), calls=%async_computation.34 | async-start | bytes 11280384 | tf_op jit(solution)/shard_map/reduce_scatter | solution.py:47
  705.4 920.1 %reduce-scatter.31.cloned.1.call-start = ((), (), s32[]{:S(2)}) async-start(), calls=%async_computation.33 | async-start | bytes 33841152 | tf_op jit(solution)/shard_map/reduce_scatter | solution.py:44
  (188 other events, 3745.9 us)
Sparse Core Ops, SparseCore 0:
  10.2 124.2 all-gather.13
  136.7 49.9 all-gather.15
  188.8 37.8 all-gather.17
  251.9 22.7 all-gather.19
  277.0 56.3 all-gather.21
  335.8 54.9 all-gather.23
  424.9 21.7 reduce-scatter.18
  448.1 22.7 all-gather.31
  472.6 22.7 all-gather.27
  517.4 21.7 reduce-scatter.26
  540.7 22.7 all-gather.35
  565.6 21.7 reduce-scatter.16
  589.6 21.7 reduce-scatter.24
  614.0 21.7 reduce-scatter.20
  638.0 21.7 reduce-scatter.28
  661.2 22.7 all-gather.25
  685.5 22.7 all-gather.33
  709.7 22.7 all-gather.29
  734.1 22.7 all-gather.37
  760.6 221.4 all-reduce.4
  986.6 65.3 reduce-scatter.36
  1056.5 119.2 reduce-scatter.34
  1180.5 119.9 reduce-scatter.32
  1305.2 320.3 reduce-scatter.30
  (2 shorter events, 40.8 us)
where the time goes:
time: 1650 us; the launch traced here: 1630 us
  waiting for transfers between devices  1160 us (70%)
  local copies, waits for them, and re-layouts  166 us (10%)
  matrix products  159 us (10%)
  blocking collectives  63.8 us (4%)
  other arithmetic  58.5 us (4%)
  between operations  18.1 us (1%)
    reduce_scatter x1, waiting for transfers between devices, scatter_every(): lax.psum_scatter(terms[0], 'dp', scatter_dimension=0, tiled=True)  325 us
    reduce_scatter x8, waiting for transfers between devices, model_total_sum(): lax.psum_scatter(partial_value, 'mp', scatter_dimension=2, tiled=True)  133 us
    reduce_scatter x1, waiting for transfers between devices, scatter_every(): lax.psum_scatter(terms[3], 'dp', scatter_dimension=0, tiled=True)  125 us
    reduce_scatter x1, waiting for transfers between devices, scatter_every(): lax.psum_scatter(terms[4], 'dp', scatter_dimension=1, tiled=True)  124 us
    all_gather x1, waiting for transfers between devices, gather_weights(): lax.all_gather(modulation_weight, 'dp', axis=0, tiled=True)  116 us
    all_gather x8, waiting for transfers between devices, model_total_sum(): return lax.all_gather(share, 'mp', axis=2, tiled=True)  79.3 us
    unnamed x28, waiting for transfers between devices  78.7 us
    psum x1, blocking collectives, body(): lax.psum((bias_sums[0], bias_sums[1], bias_sums[2], bias_sums[3], bias_su...  63.8 us
  transfers between devices with their start and end apart: 26, of which 23 were waited for; matrix products, arithmetic and copies ran while one was open for 21% of the time, Pallas kernels for 0%

commit v1 on v0

v1 whole, which is shorter than its diff:
```python
import jax
import jax.numpy as jnp
from jax import lax
from jax.sharding import PartitionSpec as P

HEAD_DIM = 72
EPSILON = 1e-06


def normalize(rows):
    center = rows - jnp.mean(rows, axis=-1, keepdims=True)
    spread = jnp.mean(center * center, axis=-1, keepdims=True)
    return center * lax.rsqrt(spread + EPSILON)


def modulated(rows, shift, scale):
    return normalize(rows) * (1.0 + scale) + shift


def gelu_tanh(values):
    return jax.nn.gelu(values, approximate=True)


def model_sum(partial):
    other = lax.ppermute(partial, "mp", [(0, 1), (1, 0)])
    return partial + other


def attention_scores(query, key_rows, keymask, scale_factor):
    scores = (
        jnp.einsum("bqhd,bkhd->bhqk", query, key_rows, preferred_element_type=jnp.float32)
        * scale_factor
    )
    return jnp.where(keymask[:, None, None, :], scores, -1e30)


def body(
    tokens,
    conditioning,
    bucket_ids,
    keep_order,
    group_counts,
    cotangent,
    modulation_weight,
    modulation_bias,
    input_weight,
    query_value_bias,
    output_weight,
    output_bias,
    expand_weight,
    expand_bias,
    shrink_weight,
    shrink_bias,
):
    f32 = jnp.float32
    bf16 = jnp.bfloat16
    batch, slots, width = tokens.shape
    keep = keep_order.shape[1]
    d_shard = modulation_weight.shape[0]
    dp_index = lax.axis_index("dp")
    scale_factor = HEAD_DIM ** (-0.5)

    lengths = jnp.where(bucket_ids == 0, slots, slots - slots // 16) // 2
    valid = jnp.where(jnp.arange(batch) < group_counts[0], lengths, 0).astype(jnp.int32)
    keymask = jnp.arange(keep)[None, :] < valid[:, None]
    rowmask = keymask[:, :, None]

    incoming_weight = lax.all_gather(input_weight, "dp", axis=1, tiled=True)
    outgoing_weight = lax.all_gather(output_weight, "dp", axis=1, tiled=True)
    expert_weight_rows = lax.all_gather(expand_weight, "dp", axis=0, tiled=True)
    narrowing_weight = lax.all_gather(shrink_weight, "dp", axis=1, tiled=True)
    inner = incoming_weight.shape[2]
    heads_here = inner // HEAD_DIM
    qv_bias = query_value_bias.astype(f32)
    outgoing_bias = output_bias.astype(f32)
    expert_bias_rows = expand_bias.astype(f32)
    narrowing_bias = shrink_bias.astype(f32)

    silu_cond = jax.nn.silu(conditioning.astype(f32)).astype(bf16)
    silu_all = lax.all_gather(silu_cond, "dp", axis=0, tiled=True)
    silu_cols = lax.dynamic_slice_in_dim(silu_all, dp_index * d_shard, d_shard, axis=1)
    mod_partial = jnp.dot(silu_cols, modulation_weight, preferred_element_type=f32)
    modulation = lax.psum_scatter(mod_partial, "dp", scatter_dimension=0, tiled=True)
    modulation = modulation + modulation_bias.astype(f32)
    pieces = modulation.reshape(batch, 6, 1, width)
    shift_one, scale_one, gate_one = (pieces[:, 0], pieces[:, 1], pieces[:, 2])
    shift_two, scale_two, gate_two = (pieces[:, 3], pieces[:, 4], pieces[:, 5])

    onehot = (keep_order[:, :, None] == jnp.arange(slots)[None, None, :]).astype(bf16)
    slot_taken = jnp.sum(onehot.astype(f32), axis=1) > 0.5
    hidden_in = jnp.einsum("brs,bsd->brd", onehot, tokens, preferred_element_type=f32)
    grad_rows = jnp.einsum("brs,bsd->brd", onehot, cotangent, preferred_element_type=f32)

    first, pull_first = jax.vjp(modulated, hidden_in, shift_one, scale_one)
    first_reduced = first.astype(bf16)
    projected_rows = jnp.einsum(
        "mzu,lug->lmzg", first_reduced, incoming_weight, preferred_element_type=f32
    )
    query = (projected_rows[0] + qv_bias[0]).astype(bf16).reshape(batch, keep, heads_here, HEAD_DIM)
    key_rows = projected_rows[1].astype(bf16).reshape(batch, keep, heads_here, HEAD_DIM)
    value = (projected_rows[2] + qv_bias[1]).astype(bf16).reshape(batch, keep, heads_here, HEAD_DIM)
    scores = attention_scores(query, key_rows, keymask, scale_factor)
    top = jnp.max(scores, axis=-1, keepdims=True)
    expo = jnp.exp(scores - top)
    total = jnp.sum(expo, axis=-1, keepdims=True)
    probs = expo / total
    log_total = top + jnp.log(total)
    attention_result = (
        jnp.einsum("bhqk,bkhd->bqhd", probs.astype(bf16), value, preferred_element_type=f32)
        .astype(bf16)
        .reshape(batch, keep, inner)
    )
    attn_out = (
        model_sum(
            jnp.einsum("hfc,cj->hfj", attention_result, outgoing_weight, preferred_element_type=f32)
        )
        + outgoing_bias
    )
    middle = hidden_in + gate_one * attn_out
    second, pull_second = jax.vjp(modulated, middle, shift_two, scale_two)
    second_reduced = second.astype(bf16)
    preactivation_rows = (
        jnp.einsum("get,tm->gem", second_reduced, expert_weight_rows, preferred_element_type=f32)
        + expert_bias_rows
    )
    activated, pull_act = jax.vjp(gelu_tanh, preactivation_rows)
    activation_reduced = activated.astype(bf16)
    mlp_out = (
        model_sum(
            jnp.einsum("xwl,lc->xwc", activation_reduced, narrowing_weight, preferred_element_type=f32)
        )
        + narrowing_bias
    )
    routed_out = jnp.where(rowmask, middle + gate_two * mlp_out, hidden_in)
    placed = jnp.einsum("brs,brd->bsd", onehot, routed_out.astype(bf16), preferred_element_type=f32)
    block_out = jnp.where(slot_taken[:, :, None], placed.astype(bf16), tokens)

    grad_final = jnp.where(rowmask, grad_rows, 0.0)
    grad_skip = grad_rows - grad_final
    grad_gate_two = jnp.sum(mlp_out * grad_final, axis=1, keepdims=True)
    grad_mlp = gate_two * grad_final
    perceptron_gradient_reduced = grad_mlp.astype(bf16)
    narrowing_term = jnp.einsum(
        "ehm,eht->mt", activation_reduced, perceptron_gradient_reduced, preferred_element_type=f32
    )
    (grad_pre,) = pull_act(
        jnp.einsum(
            "awm,hm->awh", perceptron_gradient_reduced, narrowing_weight, preferred_element_type=f32
        )
    )
    preactivation_gradient_reduced = grad_pre.astype(bf16)
    widening_term = jnp.einsum(
        "cnq,cne->qe", second_reduced, preactivation_gradient_reduced, preferred_element_type=f32
    )
    grad_second = model_sum(
        jnp.einsum(
            "pem,sm->pes", preactivation_gradient_reduced, expert_weight_rows, preferred_element_type=f32
        )
    )
    grad_middle, grad_shift_two, grad_scale_two = pull_second(grad_second)
    grad_middle = grad_middle + grad_final
    grad_gate_one = jnp.sum(attn_out * grad_middle, axis=1, keepdims=True)
    grad_attn = gate_one * grad_middle
    attention_gradient_reduced = grad_attn.astype(bf16)
    output_summand = jnp.einsum(
        "tyo,tyq->oq", attention_result, attention_gradient_reduced, preferred_element_type=f32
    )
    grad_attended = (
        jnp.einsum("znx,ox->zno", attention_gradient_reduced, outgoing_weight, preferred_element_type=f32)
        .astype(bf16)
        .reshape(batch, keep, heads_here, HEAD_DIM)
    )
    again = attention_scores(query, key_rows, keymask, scale_factor)
    probs_again = jnp.exp(again - log_total)
    grad_probs = jnp.einsum("bqhd,bkhd->bhqk", grad_attended, value, preferred_element_type=f32)
    grad_value = jnp.einsum(
        "bhqk,bqhd->bkhd", probs_again.astype(bf16), grad_attended, preferred_element_type=f32
    )
    inner_sum = jnp.sum(probs_again * grad_probs, axis=-1, keepdims=True)
    grad_scores = (probs_again * (grad_probs - inner_sum)).astype(bf16)
    grad_query = (
        jnp.einsum("bhqk,bkhd->bqhd", grad_scores, key_rows, preferred_element_type=f32) * scale_factor
    )
    grad_key = (
        jnp.einsum("bhqk,bqhd->bkhd", grad_scores, query, preferred_element_type=f32) * scale_factor
    )
    grad_proj = jnp.stack([grad_query, grad_key, grad_value]).reshape(3, batch, keep, inner)
    query_value_term = jnp.sum(grad_proj[::2], axis=(1, 2))
    projection_gradient_reduced = grad_proj.astype(bf16)
    input_summand = jnp.einsum(
        "iyj,fiyu->jfu", first_reduced, projection_gradient_reduced, preferred_element_type=f32
    )
    grad_first = model_sum(
        jnp.einsum(
            "pniu,psu->nis", projection_gradient_reduced, incoming_weight, preferred_element_type=f32
        )
    )
    grad_hidden, grad_shift_one, grad_scale_one = pull_first(grad_first)
    grad_total = grad_hidden + grad_middle + grad_skip
    placed_grad = jnp.einsum(
        "brs,brd->bsd", onehot, grad_total.astype(bf16), preferred_element_type=f32
    )
    tokens_grad = jnp.where(slot_taken[:, :, None], placed_grad.astype(bf16), cotangent)

    grad_mod = jnp.concatenate(
        [grad_shift_one, grad_scale_one, grad_gate_one, grad_shift_two, grad_scale_two, grad_gate_two],
        axis=1,
    ).reshape(batch, 6 * width)
    grad_mod_all = lax.all_gather(grad_mod.astype(bf16), "dp", axis=0, tiled=True)
    modulation_weight_grad = jnp.einsum(
        "bd,be->de", silu_cols, grad_mod_all, preferred_element_type=f32
    )

    input_weight_grad = jnp.transpose(
        lax.psum_scatter(input_summand, "dp", scatter_dimension=0, tiled=True), (1, 0, 2)
    )
    output_weight_grad = lax.psum_scatter(output_summand, "dp", scatter_dimension=1, tiled=True)
    expand_weight_grad = lax.psum_scatter(widening_term, "dp", scatter_dimension=0, tiled=True)
    shrink_weight_grad = lax.psum_scatter(narrowing_term, "dp", scatter_dimension=1, tiled=True)

    bias_sums = lax.psum(
        (
            jnp.sum(grad_mod, axis=0),
            query_value_term,
            jnp.sum(grad_attn, axis=(0, 1)),
            jnp.sum(grad_pre, axis=(0, 1)),
            jnp.sum(grad_mlp, axis=(0, 1)),
        ),
        "dp",
    )
    return (
        block_out,
        tokens_grad,
        modulation_weight_grad,
        bias_sums[0],
        input_weight_grad,
        bias_sums[1],
        output_weight_grad,
        bias_sums[2],
        expand_weight_grad,
        bias_sums[3],
        shrink_weight_grad,
        bias_sums[4],
    )


def solution(mesh):
    in_specs = (
        P("dp", None, None),
        P("dp", None),
        P("dp"),
        P("dp", None),
        P("dp"),
        P("dp", None, None),
        P("dp", None),
        P(),
        P(None, "dp", "mp"),
        P(None, "mp"),
        P("mp", "dp"),
        P(),
        P("dp", "mp"),
        P("mp"),
        P("mp", "dp"),
        P(),
    )
    out_specs = (
        P("dp", None, None),
        P("dp", None, None),
        P("dp", None),
        P(),
        P(None, "dp", "mp"),
        P(None, "mp"),
        P("mp", "dp"),
        P(),
        P("dp", "mp"),
        P("mp"),
        P("mp", "dp"),
        P(),
    )
    return jax.shard_map(body, mesh=mesh, in_specs=in_specs, out_specs=out_specs, check_vma=False)
```

time: 1650 us -> 904 us (0.55)
  waiting for transfers between devices: 1160 us -> 638 us
  local copies, waits for them, and re-layouts: 166 us -> 13.6 us
  matrix products: 159 us -> 95.1 us
  blocking collectives: 63.8 us -> 114 us
  other arithmetic: 58.5 us -> 11.6 us
    reduce_scatter x11 -> x3, waiting for transfers between devices: 707 us -> 230 us  [the longest x1 125 us: body(): lax.psum_scatter(widening_term, 'dp', scatter_dimension=0, tiled=True)]
    all_gather x13 -> x4, waiting for transfers between devices: 379 us -> 130 us  [the longest x1 52 us: body(): incoming_weight = lax.all_gather(input_weight, 'dp', axis=1, tiled=True)]
    ppermute x0 -> x4, waiting for transfers between devices: none -> 190 us  [model_sum(): other = lax.ppermute(partial, 'mp', [(0, 1), (1, 0)])]
    scatter x4 -> x0, local copies, waits for them, and re-layouts: 97.8 us -> none  [the longest x2 53.5 us: run_micro(): block_mb = tokens_mb.at[batch_rows, order_mb].set(routed_out.astype(bf16))]
    dot_general x38 -> x23, matrix products: 158 us -> 94.3 us  [the longest x1 10.5 us: body(): jnp.einsum('ehm,eht->mt', activation_reduced, perceptron_gradient_reduced...]
    all_gather x0 -> x2, blocking collectives: none -> 50.7 us  [the longest x1 27.3 us: body(): lax.all_gather(grad_mod.astype(bf16), 'dp', axis=0, tiled=True)]
    gather x8 -> x0, local copies, waits for them, and re-layouts: 19.8 us -> none  [the longest x4 11.3 us: run_micro(): jnp.take_along_axis(grad_mb, order_mb[:, :, None], axis=1)]
    unnamed x28 -> x11, waiting for transfers between devices: 78.7 us -> 88.5 us
  transfers between devices with their start and end apart: 26 -> 13, of which waited for: 23 -> 10; matrix products, arithmetic and copies ran while one was open for 21% -> 10% of each run, Pallas kernels for 0% -> 0%
where the time goes in v1:
time: 904 us; the launch traced here: 895 us
  waiting for transfers between devices  638 us (71%)
  blocking collectives  114 us (13%)
  matrix products  95.1 us (11%)
  between operations  16.1 us (2%)
  local copies, waits for them, and re-layouts  13.6 us (2%)
  other arithmetic  11.6 us (1%)
    ppermute x4, waiting for transfers between devices, model_sum(): other = lax.ppermute(partial, 'mp', [(0, 1), (1, 0)])  190 us
    reduce_scatter x1, waiting for transfers between devices, body(): lax.psum_scatter(widening_term, 'dp', scatter_dimension=0, tiled=True)  125 us
    reduce_scatter x1, waiting for transfers between devices, body(): lax.psum_scatter(narrowing_term, 'dp', scatter_dimension=1, tiled=True)  105 us
    unnamed x11, waiting for transfers between devices  88.5 us
    psum x1, blocking collectives, body(): lax.psum((jnp.sum(grad_mod, axis=0), query_value_term, jnp.sum(grad_attn,...  63 us
    all_gather x1, waiting for transfers between devices, body(): incoming_weight = lax.all_gather(input_weight, 'dp', axis=1, tiled=True)  52 us
    all_gather x1, waiting for transfers between devices, body(): narrowing_weight = lax.all_gather(shrink_weight, 'dp', axis=1, tiled=True)  46.2 us
    all_gather x1, waiting for transfers between devices, body(): outgoing_weight = lax.all_gather(output_weight, 'dp', axis=1, tiled=True)  31.4 us
  transfers between devices with their start and end apart: 13, of which 10 were waited for; matrix products, arithmetic and copies ran while one was open for 10% of the time, Pallas kernels for 0%

profile of v1, /device:TPU:0, one launch (start us, length us, event | category | flops | bytes accessed | tf_op | source)
XLA Modules:
  0.0 895.1 jit_solution(15427852965301498499)
XLA Ops:
  8.0 23.5 %all-gather = bf16[16,4,1152]{2,1,0:T(4,128)(2,1)S(1)} all-gather(bf16[1,4,1152]{2,1,0:T(4,128)(2,1)S(1)} %fusion.78), channel_id=1, replica_groups=mesh['dp'=16,'mp'=2] {'dp'}, dimensions={0}, use_global_device_ids=true | all-gather | bytes 156672 | tf_op jit(solution)/shard_map/all_gather | solution.py:80
  41.2 86.0 %all-reduce.5.cloned.1.call-done = f32[64,6912]{1,0:T(8,128)} async-done(((f32[64,6912]{1,0:T(8,128)}), f32[64,6912]{1,0:T(8,128)}) %all-reduce.5.cloned.1.call-update) | async-done | bytes 1769488
  128.4 52.0 %all-gather.7.cloned.1.call-done = bf16[3,1152,576]{2,1,0:T(8,128)(2,1)} async-done(((bf16[3,72,576]{2,1,0:T(8,128)(2,1)}), bf16[3,1152,576]{2,1,0:T(8,128)(2,1)}) %all-gather.7.cloned.1.call-update) | async-done | bytes 3981328 | tf_op jit(solution)/shard_map/all_gather | solution.py:68
  180.3 5.1 fusion.33
  189.2 31.4 %all-gather.9.cloned.1.call-done = bf16[576,1152]{0,1:T(8,128)(2,1)} async-done(((bf16[576,72]{0,1:T(8,128)(2,1)}), bf16[576,1152]{0,1:T(8,128)(2,1)}) %all-gather.9.cloned.1.call-update) | async-done | bytes 1327120 | tf_op jit(solution)/shard_map/all_gather | solution.py:69
  227.1 49.9 %collective-permute-done = f32[4,128,1152]{2,1,0:T(8,128)S(1)} collective-permute-done((f32[4,128,1152]{2,1,0:T(8,128)S(1)}, f32[4,128,1152]{2,1,0:T(8,128)S(1)}, u32[]{:S(2)}, u32[]{:S(2)}) %collective-permute-start) | collective-permute-done | bytes 2359328 | tf_op jit(solution)/shard_map/ppermute | solution.py:25
  280.2 8.8 fusion.8
  289.1 46.2 %all-gather.13.cloned.1.call-done = bf16[2304,1152]{0,1:T(8,128)(2,1)} async-done(((bf16[2304,72]{0,1:T(8,128)(2,1)}), bf16[2304,1152]{0,1:T(8,128)(2,1)}) %all-gather.13.cloned.1.call-update) | async-done | bytes 5308432 | tf_op jit(solution)/shard_map/all_gather | solution.py:71
  335.3 9.3 %fusion.93 = (f32[2304]{0:T(1024)S(1)}, bf16[4,128,2304]{2,1,0:T(8,128)(2,1)S(1)}) fusion(f32[4,128,2304]{2,1,0:T(8,128)} %fusion.8, bf16[2304,1152]{0,1:T(8,128)(2,1)} %all-gather.13.cloned.1.call-done, f32[4,128,1152]{2,1,0:T(8,128)} %fusion.59, f32[4,1152]{1,0:T(4,128)S(1)} %bitcast.143, pred[4,128]{1,0:T(4,128)(4,1)S(1)} %iota_compare_fusion.5), kind=kOutput, calls=%fused_computation.150 | convolution fusion | flops 2744448768 | bytes 14773760 | tf_op jit(solution)/shard_map/awm,hm->awh/dot_general | solution.py:147
  344.7 3.2 fusion.4
  349.5 4.1 fusion.2
  355.0 47.1 %collective-permute-done.2 = f32[4,128,1152]{2,1,0:T(8,128)S(1)} collective-permute-done((f32[4,128,1152]{2,1,0:T(8,128)S(1)}, f32[4,128,1152]{2,1,0:T(8,128)S(1)}, u32[]{:S(2)}, u32[]{:S(2)}) %collective-permute-start.2) | collective-permute-done | bytes 2359328 | tf_op jit(solution)/shard_map/ppermute | solution.py:25
  404.0 48.0 %collective-permute-done.1 = f32[4,128,1152]{2,1,0:T(8,128)S(1)} collective-permute-done((f32[4,128,1152]{2,1,0:T(8,128)S(1)}, f32[4,128,1152]{2,1,0:T(8,128)S(1)}, u32[]{:S(2)}, u32[]{:S(2)}) %collective-permute-start.1) | collective-permute-done | bytes 2359328 | tf_op jit(solution)/shard_map/ppermute | solution.py:25
  459.8 3.2 fusion.42
  468.5 6.4 convolution_bitcast_fusion.2
  475.0 10.5 %convolution_bitcast_fusion = f32[2304,1152]{0,1:T(8,128)} fusion(f32[4,128,1152]{2,1,0:T(8,128)} %fusion.59, f32[4,1152]{1,0:T(4,128)S(1)} %bitcast.145, pred[4,128]{1,0:T(4,128)(4,1)S(1)} %iota_compare_fusion.5, f32[4,128,2304]{2,1,0:T(8,128)} %fusion.8), kind=kOutput, calls=%fused_computation | convolution fusion | flops 2730295296 | bytes 17713664 | tf_op jit(solution)/shard_map/ehm,eht->mt/dot_general | solution.py:143
  485.7 9.4 %convolution_bitcast_fusion.1 = f32[1152,2304]{1,0:T(8,128)} fusion(bf16[4,128,2304]{2,1,0:T(8,128)(2,1)} %copy-done.43, f32[4,128,1152]{2,1,0:T(8,128)} %copy-done.2, f32[4,1152]{1,0:T(4,128)S(1)} %get-tuple-element.57, f32[4,1152]{1,0:T(4,128)S(1)} %get-tuple-element.58, f32[4,128]{1,0:T(4,128)S(1)} %fusion.80, f32[4,128]{1,0:T(4,128)S(1)} %broadcast_multiply_fusion), kind=kOutput, calls=%fused_computation.1 | convolution fusion | flops 2720858112 | bytes 15376384 | tf_op jit(solution)/shard_map/cnq,cne->qe/dot_general | solution.py:152
  495.2 6.6 fusion.25
  509.9 44.8 %collective-permute-done.3 = f32[4,128,1152]{2,1,0:T(8,128)S(1)} collective-permute-done((f32[4,128,1152]{2,1,0:T(8,128)S(1)}, f32[4,128,1152]{2,1,0:T(8,128)S(1)}, u32[]{:S(2)}, u32[]{:S(2)}) %collective-permute-start.3) | collective-permute-done | bytes 2359328 | tf_op jit(solution)/shard_map/ppermute | solution.py:25
  557.1 27.3 %all-gather.1 = bf16[16,4,6912]{2,1,0:T(4,128)(2,1)} all-gather(bf16[1,4,6912]{2,1,0:T(4,128)(2,1)S(1)} %reshape.202), channel_id=1, replica_groups=mesh['dp'=16,'mp'=2] {'dp'}, dimensions={0}, use_global_device_ids=true | all-gather | bytes 940032 | tf_op jit(solution)/shard_map/all_gather | solution.py:209
  586.0 63.0 %all-reduce.2 = (f32[6912]{0:T(1024)}, f32[2,576]{1,0:T(2,128)}, f32[1152]{0:T(1024)}, f32[2304]{0:T(1024)}, f32[1152]{0:T(1024)}) all-reduce(f32[6912]{0:T(1024)S(1)} %reduce_sum.234, f32[2,576]{1,0:T(2,128)S(1)} %slice_reduce_fusion, f32[1152]{0:T(1024)S(1)} %get-tuple-element.39, ...), channel_id=1, replica_groups=mesh['dp'=16,'mp'=2] {'dp'}, use_global_device_ids=true, to_apply=%region_20.21 | all-reduce | flops 12672 | bytes 101376 | tf_op jit(solution)/shard_map/psum | solution.py:221
  651.1 7.4 fusion.24
  658.5 105.2 %reduce-scatter.11.cloned.1.call-done = f32[2304,72]{0,1:T(8,128)} async-done(((f32[2304,1152]{0,1:T(8,128)}), f32[2304,72]{0,1:T(8,128)}) %reduce-scatter.11.cloned.1.call-update) | async-done | bytes 663568 | tf_op jit(solution)/shard_map/reduce_scatter | solution.py:219
  763.7 124.6 %reduce-scatter.9.cloned.1.call-done = f32[72,2304]{1,0:T(8,128)} async-done(((f32[1152,2304]{1,0:T(8,128)}), f32[72,2304]{1,0:T(8,128)}) %reduce-scatter.9.cloned.1.call-update) | async-done | bytes 663568 | tf_op jit(solution)/shard_map/reduce_scatter | solution.py:218
  (183 shorter events, 55.9 us)
Async XLA Ops:
  7.2 24.4 %copy-start = (bf16[72,6912]{1,0:T(8,128)(2,1)S(1)}, bf16[72,6912]{1,0:T(8,128)(2,1)}, u32[]{:S(2)}) copy-start(bf16[72,6912]{1,0:T(8,128)(2,1)} %param.22) | copy-start | bytes 2985988
  7.2 120.0 %all-reduce.5.cloned.1.call-start = ((), (), s32[]{:S(2)}) async-start(), calls=%async_computation.11 | async-start | bytes 3538944
  33.3 147.0 %all-gather.7.cloned.1.call-start = ((), (), s32[]{:S(2)}) async-start(), calls=%async_computation.4 | async-start | bytes 4700160 | tf_op jit(solution)/shard_map/all_gather | solution.py:68
  34.0 186.6 %all-gather.9.cloned.1.call-start = ((), (), s32[]{:S(2)}) async-start(), calls=%async_computation.5 | async-start | bytes 1566720 | tf_op jit(solution)/shard_map/all_gather | solution.py:69
  34.8 245.4 %all-gather.11.cloned.1.call-start = ((), (), s32[]{:S(2)}) async-start(), calls=%async_computation.6 | async-start | bytes 5640192 | tf_op jit(solution)/shard_map/all_gather | solution.py:70
  35.4 299.9 %all-gather.13.cloned.1.call-start = ((), (), s32[]{:S(2)}) async-start(), calls=%async_computation.7 | async-start | bytes 5640192 | tf_op jit(solution)/shard_map/all_gather | solution.py:71
  35.9 622.5 %reduce-scatter.13.cloned.1.call-start = ((), (), s32[]{:S(2)}) async-start(), calls=%async_computation.12 | async-start | bytes 3133440
  189.2 35.9 %copy-start.35 = (bf16[1152]{0:T(1024)(128)(2,1)S(1)}, bf16[1152]{0:T(1024)(128)(2,1)}, u32[]{:S(2)}) copy-start(bf16[1152]{0:T(1024)(128)(2,1)} %param.27) | copy-start | bytes 6916
  189.2 35.9 %copy-start.34 = (bf16[2304]{0:T(1024)(128)(2,1)S(1)}, bf16[2304]{0:T(1024)(128)(2,1)}, u32[]{:S(2)}) copy-start(bf16[2304]{0:T(1024)(128)(2,1)} %param.29) | copy-start | bytes 13828
  223.5 53.5 %copy-start.13 = (f32[4,128,1152]{2,1,0:T(8,128)}, f32[4,128,1152]{2,1,0:T(8,128)S(1)}, u32[]{:S(2)}) copy-start(f32[4,128,1152]{2,1,0:T(8,128)S(1)} %fusion.40) | copy-start | bytes 7077892
  223.5 53.5 %collective-permute-start = (f32[4,128,1152]{2,1,0:T(8,128)S(1)}, f32[4,128,1152]{2,1,0:T(8,128)S(1)}, u32[]{:S(2)}, u32[]{:S(2)}) collective-permute-start(f32[4,128,1152]{2,1,0:T(8,128)S(1)} %fusion.40), channel_id=1, source_target_pairs={{0,1},{1,0},{2,3},{3,2},{4,5},{5,4},{6,7},{7,6},{8,9},{9,8},{10,11... | collective-permute-start | bytes 7077896 | tf_op jit(solution)/shard_map/ppermute | solution.py:25
  347.9 54.2 %copy-start.3 = (f32[4,128,1152]{2,1,0:T(8,128)S(1)}, f32[4,128,1152]{2,1,0:T(8,128)}, u32[]{:S(2)}) copy-start(f32[4,128,1152]{2,1,0:T(8,128)} %copy-done.2) | copy-start | bytes 7077892
  348.0 54.1 %collective-permute-start.2 = (f32[4,128,1152]{2,1,0:T(8,128)S(1)}, f32[4,128,1152]{2,1,0:T(8,128)S(1)}, u32[]{:S(2)}, u32[]{:S(2)}) collective-permute-start(f32[4,128,1152]{2,1,0:T(8,128)S(1)} %fusion.4), channel_id=1, source_target_pairs={{0,1},{1,0},{2,3},{3,2},{4,5},{5,4},{6,7},{7,6},{8,9},{9,8},{10,11... | collective-permute-start | bytes 7077896 | tf_op jit(solution)/shard_map/ppermute | solution.py:25
  353.6 98.4 %copy-start.19 = (f32[4,128,1152]{2,1,0:T(8,128)}, f32[4,128,1152]{2,1,0:T(8,128)S(1)}, u32[]{:S(2)}) copy-start(f32[4,128,1152]{2,1,0:T(8,128)S(1)} %fusion.2) | copy-start | bytes 7077892
  353.6 98.4 %collective-permute-start.1 = (f32[4,128,1152]{2,1,0:T(8,128)S(1)}, f32[4,128,1152]{2,1,0:T(8,128)S(1)}, u32[]{:S(2)}, u32[]{:S(2)}) collective-permute-start(f32[4,128,1152]{2,1,0:T(8,128)S(1)} %fusion.2), channel_id=1, source_target_pairs={{0,1},{1,0},{2,3},{3,2},{4,5},{5,4},{6,7},{7,6},{8,9},{9,8},{10,11... | collective-permute-start | bytes 7077896 | tf_op jit(solution)/shard_map/ppermute | solution.py:25
  402.1 49.9 %copy-start.16 = (f32[4,128,1152]{2,1,0:T(8,128)S(1)}, f32[4,128,1152]{2,1,0:T(8,128)}, u32[]{:S(2)}) copy-start(f32[4,128,1152]{2,1,0:T(8,128)} %copy-done.15) | copy-start | bytes 7077892
  402.7 49.3 %copy-start.9 = (f32[4,128,1152]{2,1,0:T(8,128)S(1)}, f32[4,128,1152]{2,1,0:T(8,128)}, u32[]{:S(2)}) copy-start(f32[4,128,1152]{2,1,0:T(8,128)} %fusion.59) | copy-start | bytes 7077892
  402.7 49.3 %copy-start.14 = (f32[4,128,1152]{2,1,0:T(8,128)S(1)}, f32[4,128,1152]{2,1,0:T(8,128)}, u32[]{:S(2)}) copy-start(f32[4,128,1152]{2,1,0:T(8,128)} %copy-done.13) | copy-start | bytes 7077892
  403.9 52.5 %copy-start.31 = (bf16[4,8,72,128]{3,2,1,0:T(8,128)(2,1)S(1)}, bf16[4,8,72,128]{3,2,1,0:T(8,128)(2,1)}, u32[]{:S(2)}) copy-start(bf16[4,8,72,128]{3,2,1,0:T(8,128)(2,1)} %convolution_convert_fusion.2) | copy-start | bytes 1769476
  459.3 199.2 %reduce-scatter.7.cloned.1.call-start = ((), (), s32[]{:S(2)}) async-start(), calls=%async_computation.8 | async-start | bytes 9400320 | tf_op jit(solution)/shard_map/reduce_scatter | solution.py:215
  474.9 288.7 %reduce-scatter.11.cloned.1.call-start = ((), (), s32[]{:S(2)}) async-start(), calls=%async_computation.10 | async-start | bytes 11280384 | tf_op jit(solution)/shard_map/reduce_scatter | solution.py:219
  485.5 402.8 %reduce-scatter.9.cloned.1.call-start = ((), (), s32[]{:S(2)}) async-start(), calls=%async_computation.9 | async-start | bytes 11280384 | tf_op jit(solution)/shard_map/reduce_scatter | solution.py:218
  501.7 53.0 %collective-permute-start.3 = (f32[4,128,1152]{2,1,0:T(8,128)S(1)}, f32[4,128,1152]{2,1,0:T(8,128)S(1)}, u32[]{:S(2)}, u32[]{:S(2)}) collective-permute-start(f32[4,128,1152]{2,1,0:T(8,128)S(1)} %fusion.25), channel_id=1, source_target_pairs={{0,1},{1,0},{2,3},{3,2},{4,5},{5,4},{6,7},{7,6},{8,9},{9,8},{10,11... | collective-permute-start | bytes 7077896 | tf_op jit(solution)/shard_map/ppermute | solution.py:25
  651.1 237.2 %copy-start.1 = (bf16[72,6912]{1,0:T(8,128)(2,1)S(1)}, bf16[72,6912]{1,0:T(8,128)(2,1)}, u32[]{:S(2)}) copy-start(bf16[72,6912]{1,0:T(8,128)(2,1)} %param.22) | copy-start | bytes 2985988
  (33 other events, 119.3 us)
Sparse Core Ops, SparseCore 0:
  33.4 93.7 all-reduce.4
  129.7 50.6 all-gather.6
  182.7 37.8 all-gather.8
  222.9 55.1 all-gather.10
  280.3 54.9 all-gather.12
  459.4 63.8 reduce-scatter.12
  528.5 111.0 reduce-scatter.6
  644.3 119.3 reduce-scatter.10
  768.3 119.9 reduce-scatter.8

commit v2 on v1

--- a/solution.py
+++ b/solution.py
@@ -1,3 +1,5 @@
+import functools
+
 import jax
 import jax.numpy as jnp
 from jax import lax
@@ -26,6 +28,101 @@
     return partial + other
 
 
+def chip_ring(mesh):
+    devices = mesh.devices
+    chips = devices.shape[0] // 2
+    try:
+        coords = [tuple(devices[2 * k, 0].coords) for k in range(chips)]
+    except (AttributeError, TypeError):
+        return None
+    varying = [a for a in range(len(coords[0])) if len({c[a] for c in coords}) > 1]
+    if len(varying) != 2 or chips < 4 or chips > 8:
+        return None
+    sizes = [len({c[a] for c in coords}) for a in varying]
+    if 2 not in sizes:
+        return None
+    short, long = (varying[0], varying[1]) if sizes[0] == 2 else (varying[1], varying[0])
+    low_short = min(c[short] for c in coords)
+    up = sorted((k for k in range(chips) if coords[k][short] == low_short), key=lambda k: coords[k][long])
+    down = sorted((k for k in range(chips) if coords[k][short] != low_short), key=lambda k: -coords[k][long])
+    return up + down
+
+
+class Ring:
+    def __init__(self, order):
+        self.native = order is None
+        if self.native:
+            return
+        self.order = order
+        self.n = len(order)
+        position = [0] * self.n
+        for p, k in enumerate(order):
+            position[k] = p
+        self.position = position
+
+        def step(direction):
+            pairs = []
+            for p, k in enumerate(order):
+                nxt = order[(p + direction) % self.n]
+                for c in range(2):
+                    pairs.append((2 * k + c, 2 * nxt + c))
+            return pairs
+
+        self.forward = step(1)
+        self.backward = step(-1)
+        self.swap = [(2 * k + c, 2 * k + 1 - c) for k in range(self.n) for c in range(2)]
+
+    def place(self):
+        index = lax.axis_index("dp")
+        chip = index // 2
+        core = index % 2
+        p = jnp.asarray(self.position, jnp.int32)[chip]
+        return chip, core, p
+
+    def gather(self, shard, split_axis):
+        if self.native:
+            return lax.all_gather(shard, "dp", axis=0, tiled=False)
+        n = self.n
+        chip, core, p = self.place()
+        a, b = jnp.split(shard, 2, axis=split_axis)
+        got_a, got_b = [a], [b]
+        for _ in range(1, n):
+            a = lax.ppermute(a, "dp", self.forward)
+            b = lax.ppermute(b, "dp", self.backward)
+            got_a.append(a)
+            got_b.append(b)
+        positions = jnp.asarray(self.position, jnp.int32)
+        from_a = jnp.take(jnp.stack(got_a), (p - positions) % n, axis=0)
+        from_b = jnp.take(jnp.stack(got_b), (positions - p) % n, axis=0)
+        mine = jnp.concatenate([from_a, from_b], axis=split_axis + 1)
+        other = lax.ppermute(mine, "dp", self.swap)
+        pair = jnp.stack([mine, other], axis=1)
+        pair = jnp.take(pair, jnp.stack([core, 1 - core]), axis=1)
+        return pair.reshape((2 * n,) + shard.shape)
+
+    def reduce(self, blocks, split_axis, wire):
+        if self.native:
+            return lax.psum_scatter(blocks, "dp", scatter_dimension=0, tiled=False)
+        n = self.n
+        chip, core, p = self.place()
+        order = jnp.asarray(self.order, jnp.int32)
+        paired = blocks.reshape((n, 2) + blocks.shape[1:])
+        mine = jnp.take(paired, core, axis=1)
+        theirs = jnp.take(paired, 1 - core, axis=1)
+        summed = mine + lax.ppermute(theirs, "dp", self.swap)
+        half_a, half_b = jnp.split(summed, 2, axis=split_axis + 1)
+        results = []
+        for half, perm, sign in ((half_a, self.forward, 1), (half_b, self.backward, -1)):
+            carried = None
+            for t in range(1, n):
+                own = lax.dynamic_index_in_dim(half, order[(p - sign * t) % n], axis=0, keepdims=False)
+                total = own if carried is None else carried + own
+                carried = lax.ppermute(total.astype(wire), "dp", perm).astype(jnp.float32)
+            own = lax.dynamic_index_in_dim(half, chip, axis=0, keepdims=False)
+            results.append(carried + own)
+        return jnp.concatenate(results, axis=split_axis)
+
+
 def attention_scores(query, key_rows, keymask, scale_factor):
     scores = (
         jnp.einsum("bqhd,bkhd->bhqk", query, key_rows, preferred_element_type=jnp.float32)
@@ -35,6 +132,7 @@
 
 
 def body(
+    ring,
     tokens,
     conditioning,
     bucket_ids,
@@ -57,6 +155,7 @@
     batch, slots, width = tokens.shape
     keep = keep_order.shape[1]
     d_shard = modulation_weight.shape[0]
+    n_dp = width // d_shard
     dp_index = lax.axis_index("dp")
     scale_factor = HEAD_DIM ** (-0.5)
 
@@ -65,11 +164,11 @@
     keymask = jnp.arange(keep)[None, :] < valid[:, None]
     rowmask = keymask[:, :, None]
 
-    incoming_weight = lax.all_gather(input_weight, "dp", axis=1, tiled=True)
-    outgoing_weight = lax.all_gather(output_weight, "dp", axis=1, tiled=True)
-    expert_weight_rows = lax.all_gather(expand_weight, "dp", axis=0, tiled=True)
-    narrowing_weight = lax.all_gather(shrink_weight, "dp", axis=1, tiled=True)
-    inner = incoming_weight.shape[2]
+    incoming_weight = ring.gather(input_weight, 2)
+    outgoing_weight = ring.gather(output_weight, 0)
+    expert_weight_rows = ring.gather(expand_weight, 1).reshape(width, -1)
+    narrowing_weight = ring.gather(shrink_weight, 0)
+    inner = incoming_weight.shape[3]
     heads_here = inner // HEAD_DIM
     qv_bias = query_value_bias.astype(f32)
     outgoing_bias = output_bias.astype(f32)
@@ -77,10 +176,10 @@
     narrowing_bias = shrink_bias.astype(f32)
 
     silu_cond = jax.nn.silu(conditioning.astype(f32)).astype(bf16)
-    silu_all = lax.all_gather(silu_cond, "dp", axis=0, tiled=True)
+    silu_all = ring.gather(silu_cond, 1).reshape(-1, width)
     silu_cols = lax.dynamic_slice_in_dim(silu_all, dp_index * d_shard, d_shard, axis=1)
     mod_partial = jnp.dot(silu_cols, modulation_weight, preferred_element_type=f32)
-    modulation = lax.psum_scatter(mod_partial, "dp", scatter_dimension=0, tiled=True)
+    modulation = ring.reduce(mod_partial.reshape(n_dp, batch, -1), 1, f32)
     modulation = modulation + modulation_bias.astype(f32)
     pieces = modulation.reshape(batch, 6, 1, width)
     shift_one, scale_one, gate_one = (pieces[:, 0], pieces[:, 1], pieces[:, 2])
@@ -91,10 +190,13 @@
     hidden_in = jnp.einsum("brs,bsd->brd", onehot, tokens, preferred_element_type=f32)
     grad_rows = jnp.einsum("brs,bsd->brd", onehot, cotangent, preferred_element_type=f32)
 
+    def blocks(rows):
+        return rows.reshape(batch, keep, n_dp, d_shard)
+
     first, pull_first = jax.vjp(modulated, hidden_in, shift_one, scale_one)
     first_reduced = first.astype(bf16)
     projected_rows = jnp.einsum(
-        "mzu,lug->lmzg", first_reduced, incoming_weight, preferred_element_type=f32
+        "bkdr,dlru->lbku", blocks(first_reduced), incoming_weight, preferred_element_type=f32
     )
     query = (projected_rows[0] + qv_bias[0]).astype(bf16).reshape(batch, keep, heads_here, HEAD_DIM)
     key_rows = projected_rows[1].astype(bf16).reshape(batch, keep, heads_here, HEAD_DIM)
@@ -112,7 +214,9 @@
     )
     attn_out = (
         model_sum(
-            jnp.einsum("hfc,cj->hfj", attention_result, outgoing_weight, preferred_element_type=f32)
+            jnp.einsum(
+                "bkh,dhr->bkdr", attention_result, outgoing_weight, preferred_element_type=f32
+            ).reshape(batch, keep, width)
         )
         + outgoing_bias
     )
@@ -127,7 +231,9 @@
     activation_reduced = activated.astype(bf16)
     mlp_out = (
         model_sum(
-            jnp.einsum("xwl,lc->xwc", activation_reduced, narrowing_weight, preferred_element_type=f32)
+            jnp.einsum(
+                "bku,dur->bkdr", activation_reduced, narrowing_weight, preferred_element_type=f32
+            ).reshape(batch, keep, width)
         )
         + narrowing_bias
     )
@@ -141,17 +247,19 @@
     grad_mlp = gate_two * grad_final
     perceptron_gradient_reduced = grad_mlp.astype(bf16)
     narrowing_term = jnp.einsum(
-        "ehm,eht->mt", activation_reduced, perceptron_gradient_reduced, preferred_element_type=f32
-    )
+        "bku,bkdr->dur", activation_reduced, blocks(perceptron_gradient_reduced), preferred_element_type=f32
+    )
+    shrink_weight_grad = ring.reduce(narrowing_term, 0, bf16)
     (grad_pre,) = pull_act(
         jnp.einsum(
-            "awm,hm->awh", perceptron_gradient_reduced, narrowing_weight, preferred_element_type=f32
+            "bkdr,dur->bku", blocks(perceptron_gradient_reduced), narrowing_weight, preferred_element_type=f32
         )
     )
     preactivation_gradient_reduced = grad_pre.astype(bf16)
     widening_term = jnp.einsum(
         "cnq,cne->qe", second_reduced, preactivation_gradient_reduced, preferred_element_type=f32
     )
+    expand_weight_grad = ring.reduce(widening_term.reshape(n_dp, d_shard, -1), 1, bf16)
     grad_second = model_sum(
         jnp.einsum(
             "pem,sm->pes", preactivation_gradient_reduced, expert_weight_rows, preferred_element_type=f32
@@ -163,10 +271,13 @@
     grad_attn = gate_one * grad_middle
     attention_gradient_reduced = grad_attn.astype(bf16)
     output_summand = jnp.einsum(
-        "tyo,tyq->oq", attention_result, attention_gradient_reduced, preferred_element_type=f32
-    )
+        "bkh,bkdr->dhr", attention_result, blocks(attention_gradient_reduced), preferred_element_type=f32
+    )
+    output_weight_grad = ring.reduce(output_summand, 0, bf16)
     grad_attended = (
-        jnp.einsum("znx,ox->zno", attention_gradient_reduced, outgoing_weight, preferred_element_type=f32)
+        jnp.einsum(
+            "bkdr,dhr->bkh", blocks(attention_gradient_reduced), outgoing_weight, preferred_element_type=f32
+        )
         .astype(bf16)
         .reshape(batch, keep, heads_here, HEAD_DIM)
     )
@@ -188,12 +299,13 @@
     query_value_term = jnp.sum(grad_proj[::2], axis=(1, 2))
     projection_gradient_reduced = grad_proj.astype(bf16)
     input_summand = jnp.einsum(
-        "iyj,fiyu->jfu", first_reduced, projection_gradient_reduced, preferred_element_type=f32
-    )
+        "bkdr,lbku->dlru", blocks(first_reduced), projection_gradient_reduced, preferred_element_type=f32
+    )
+    input_weight_grad = ring.reduce(input_summand, 2, bf16)
     grad_first = model_sum(
         jnp.einsum(
-            "pniu,psu->nis", projection_gradient_reduced, incoming_weight, preferred_element_type=f32
-        )
+            "lbku,dlru->bkdr", projection_gradient_reduced, incoming_weight, preferred_element_type=f32
+        ).reshape(batch, keep, width)
     )
     grad_hidden, grad_shift_one, grad_scale_one = pull_first(grad_first)
     grad_total = grad_hidden + grad_middle + grad_skip
@@ -206,35 +318,30 @@
         [grad_shift_one, grad_scale_one, grad_gate_one, grad_shift_two, grad_scale_two, grad_gate_two],
         axis=1,
     ).reshape(batch, 6 * width)
-    grad_mod_all = lax.all_gather(grad_mod.astype(bf16), "dp", axis=0, tiled=True)
+    bias_terms = (
+        jnp.sum(grad_mod, axis=0),
+        query_value_term.reshape(-1),
+        jnp.sum(grad_attn, axis=(0, 1)),
+        jnp.sum(grad_pre, axis=(0, 1)),
+        jnp.sum(grad_mlp, axis=(0, 1)),
+    )
+    gathered = ring.gather(jnp.concatenate((grad_mod.reshape(-1),) + bias_terms), 0)
+    grad_mod_all = gathered[:, : grad_mod.size].reshape(-1, 6 * width).astype(bf16)
     modulation_weight_grad = jnp.einsum(
         "bd,be->de", silu_cols, grad_mod_all, preferred_element_type=f32
     )
-
-    input_weight_grad = jnp.transpose(
-        lax.psum_scatter(input_summand, "dp", scatter_dimension=0, tiled=True), (1, 0, 2)
-    )
-    output_weight_grad = lax.psum_scatter(output_summand, "dp", scatter_dimension=1, tiled=True)
-    expand_weight_grad = lax.psum_scatter(widening_term, "dp", scatter_dimension=0, tiled=True)
-    shrink_weight_grad = lax.psum_scatter(narrowing_term, "dp", scatter_dimension=1, tiled=True)
-
-    bias_sums = lax.psum(
-        (
-            jnp.sum(grad_mod, axis=0),
-            query_value_term,
-            jnp.sum(grad_attn, axis=(0, 1)),
-            jnp.sum(grad_pre, axis=(0, 1)),
-            jnp.sum(grad_mlp, axis=(0, 1)),
-        ),
-        "dp",
-    )
+    bias_sums = []
+    offset = grad_mod.size
+    for term in bias_terms:
+        bias_sums.append(jnp.sum(gathered[:, offset : offset + term.size], axis=0))
+        offset += term.size
     return (
         block_out,
         tokens_grad,
         modulation_weight_grad,
         bias_sums[0],
         input_weight_grad,
-        bias_sums[1],
+        bias_sums[1].reshape(query_value_term.shape),
         output_weight_grad,
         bias_sums[2],
         expand_weight_grad,
@@ -277,4 +384,4 @@
         P("mp", "dp"),
         P(),
     )
-    return jax.shard_map(body, mesh=mesh, in_specs=in_specs, out_specs=out_specs, check_vma=False)
+    return jax.shard_map(functools.partial(body, Ring(chip_ring(mesh))), mesh=mesh, in_specs=in_specs, out_specs=out_specs, check_vma=False)

time: 904 us -> 860 us (0.951)
  waiting for transfers between devices: 638 us -> 215 us
  local copies, waits for them, and re-layouts: 13.6 us -> 201 us
  starting transfers between devices: 7.07 us -> 190 us
  other arithmetic: 11.6 us -> 126 us
  blocking collectives: 114 us -> 0 us
  between operations: 16.1 us -> 39.5 us
  matrix products: 95.1 us -> 75.7 us
    reduce_scatter x3 -> x0, waiting for transfers between devices: 230 us -> none  [the longest x1 125 us: body(): lax.psum_scatter(widening_term, 'dp', scatter_dimension=0, tiled=True)]
    ppermute x0 -> x165, starting transfers between devices: none -> 184 us  [the longest x70 76.8 us: reduce(): carried = lax.ppermute(total.astype(wire), 'dp', perm).astype(jnp.float32)]
    ppermute x0 -> x165, waiting for transfers between devices: none -> 132 us  [the longest x70 80.1 us: reduce(): carried = lax.ppermute(total.astype(wire), 'dp', perm).astype(jnp.float32)]
    all_gather x4 -> x0, waiting for transfers between devices: 130 us -> none  [the longest x1 52 us: body(): incoming_weight = lax.all_gather(input_weight, 'dp', axis=1, tiled=True)]
    ppermute x4, waiting for transfers between devices: 190 us -> 82.3 us  [model_sum(): other = lax.ppermute(partial, 'mp', [(0, 1), (1, 0)])]
    unnamed x11 -> x0, waiting for transfers between devices: 88.5 us -> none
    unnamed x97 -> x303, local copies, waits for them, and re-layouts: 12.9 us -> 79.5 us
    gather x0 -> x26, local copies, waits for them, and re-layouts: none -> 65.3 us  [the longest x14 40 us: gather(): pair = jnp.take(pair, jnp.stack([core, 1 - core]), axis=1)]
  transfers between devices with their start and end apart: 13 -> 169, of which waited for: 10 -> 89; matrix products, arithmetic and copies ran while one was open for 10% -> 41% of each run, Pallas kernels for 0% -> 0%
where the time goes in v2:
time: 860 us; the launch traced here: 847 us
  waiting for transfers between devices  215 us (25%)
  local copies, waits for them, and re-layouts  201 us (23%)
  starting transfers between devices  190 us (22%)
  other arithmetic  126 us (15%)
  matrix products  75.7 us (9%)
  between operations  39.5 us (5%)
    ppermute x4, waiting for transfers between devices, model_sum(): other = lax.ppermute(partial, 'mp', [(0, 1), (1, 0)])  82.3 us
    ppermute x70, waiting for transfers between devices, reduce(): carried = lax.ppermute(total.astype(wire), 'dp', perm).astype(jnp.float32)  80.1 us
    unnamed x303, local copies, waits for them, and re-layouts  79.5 us
    ppermute x70, starting transfers between devices, reduce(): carried = lax.ppermute(total.astype(wire), 'dp', perm).astype(jnp.float32)  76.8 us
    ppermute x42, starting transfers between devices, gather(): a = lax.ppermute(a, 'dp', self.forward)  69.1 us
    gather x14, local copies, waits for them, and re-layouts, gather(): pair = jnp.take(pair, jnp.stack([core, 1 - core]), axis=1)  40 us
    ppermute x42, starting transfers between devices, gather(): b = lax.ppermute(b, 'dp', self.backward)  36.7 us
    ppermute x42, waiting for transfers between devices, gather(): b = lax.ppermute(b, 'dp', self.backward)  32.9 us
  transfers between devices with their start and end apart: 169, of which 89 were waited for; matrix products, arithmetic and copies ran while one was open for 41% of the time, Pallas kernels for 0%

profile of v2, /device:TPU:0, one launch (start us, length us, event | category | flops | bytes accessed | tf_op | source)
XLA Modules:
  0.0 847.1 jit_solution(15840232136495702915)
XLA Ops:
  361.3 4.1 gather_fusion.3
  368.8 4.7 pad_maximum_fusion.2
  389.0 4.1 gather_fusion.7
  393.2 4.1 gather_fusion.8
  397.2 4.3 fusion.28
  401.5 4.1 gather_fusion.5
  405.7 4.1 gather_fusion.6
  409.8 4.3 broadcast_select_fusion
  422.6 11.0 %collective-permute-done.60 = f32[4,128,1152]{2,1,0:T(8,128)} collective-permute-done((f32[4,128,1152]{2,1,0:T(8,128)}, f32[4,128,1152]{2,1,0:T(8,128)}, u32[]{:S(2)}, u32[]{:S(2)}) %collective-permute-start.60) | collective-permute-done | bytes 2359328 | tf_op jit(solution)/shard_map/ppermute | solution.py:27
  440.9 4.1 fusion.150
  454.8 39.1 %collective-permute-done.91 = f32[4,128,1152]{2,1,0:T(8,128)S(1)} collective-permute-done((f32[4,128,1152]{2,1,0:T(8,128)S(1)}, f32[4,128,1152]{2,1,0:T(8,128)S(1)}, u32[]{:S(2)}, u32[]{:S(2)}) %collective-permute-start.91) | collective-permute-done | bytes 2359328 | tf_op jit(solution)/shard_map/ppermute | solution.py:27
  499.8 9.9 %fusion.166 = (f32[2304]{0:T(1024)}, bf16[4,128,2304]{2,1,0:T(8,128)(2,1)S(1)}) fusion(f32[4,128,2304]{2,1,0:T(8,128)} %copy-done.103, bf16[4,128,16,72]{1,3,2,0:T(8,128)(2,1)} %bitcast.764, bf16[16,2304,72,1]{1,2,0,3:T(8,128)(2,1)} %bitcast.749), kind=kOutput, calls=%fused_computation.496 | convolution fusion | flops 2742679296 | bytes 13575168 | tf_op jit(solution)/shard_map/bkdr,dur->bku/dot_general | solution.py:254
  509.7 5.9 fusion.6
  517.1 5.5 fusion.32
  534.8 4.7 copy-done.15
  542.4 21.1 %collective-permute-done.92 = f32[4,128,1152]{2,1,0:T(8,128)S(1)} collective-permute-done((f32[4,128,1152]{2,1,0:T(8,128)S(1)}, f32[4,128,1152]{2,1,0:T(8,128)S(1)}, u32[]{:S(2)}, u32[]{:S(2)}) %collective-permute-start.92) | collective-permute-done | bytes 2359328 | tf_op jit(solution)/shard_map/ppermute | solution.py:27
  565.8 4.0 multiply_reduce_fusion.7
  583.7 4.4 convolution_bitcast_fusion.1
  594.4 5.0 fusion.40
  634.8 11.2 %collective-permute-done.93 = f32[4,128,1152]{2,1,0:T(8,128)} collective-permute-done((f32[4,128,1152]{2,1,0:T(8,128)}, f32[4,128,1152]{2,1,0:T(8,128)}, u32[]{:S(2)}, u32[]{:S(2)}) %collective-permute-start.93) | collective-permute-done | bytes 2359328 | tf_op jit(solution)/shard_map/ppermute | solution.py:27
  688.1 7.0 fusion.25
  706.9 4.9 fusion.2
  774.5 4.9 collective-permute-done.117
  779.8 4.9 collective-permute-done.110
  (921 shorter events, 626.2 us)
Async XLA Ops:
  2.1 65.1 %collective-permute-start = (bf16[4,576]{1,0:T(4,128)(2,1)}, bf16[4,576]{1,0:T(4,128)(2,1)}, u32[]{:S(2)}, u32[]{:S(2)}) collective-permute-start(bf16[4,576]{1,0:T(4,128)(2,1)} %get-tuple-element.153), channel_id=1, source_target_pairs={{0,8},{2,10},{8,16},{10,18},{16,24},{18,26},{24,28},{26,30},{28,20... | collective-permute-start | bytes 13832 | tf_op jit(solution)/shard_map/ppermute | solution.py:90
  5.2 62.8 %collective-permute-start.7 = (bf16[4,576]{1,0:T(4,128)(2,1)S(1)}, bf16[4,576]{1,0:T(4,128)(2,1)}, u32[]{:S(2)}, u32[]{:S(2)}) collective-permute-start(bf16[4,576]{1,0:T(4,128)(2,1)S(1)} %get-tuple-element.154), channel_id=1, source_target_pairs={{0,4},{2,6},{8,0},{10,2},{16,8},{18,10},{24,16},{26,18},{28,24},{3... | collective-permute-start | bytes 13832 | tf_op jit(solution)/shard_map/ppermute | solution.py:91
  6.7 110.4 %collective-permute-start.45 = (bf16[288,72]{0,1:T(8,128)(2,1)}, bf16[288,72]{0,1:T(8,128)(2,1)}, u32[]{:S(2)}, u32[]{:S(2)}) collective-permute-start(bf16[288,72]{0,1:T(8,128)(2,1)} %get-tuple-element.149), channel_id=1, source_target_pairs={{0,8},{2,10},{8,16},{10,18},{16,24},{18,26},{24,28},{26,30},{28,20... | collective-permute-start | bytes 124424 | tf_op jit(solution)/shard_map/ppermute | solution.py:90
  8.7 109.9 %collective-permute-start.52 = (bf16[288,72]{0,1:T(8,128)(2,1)S(1)}, bf16[288,72]{0,1:T(8,128)(2,1)}, u32[]{:S(2)}, u32[]{:S(2)}) collective-permute-start(bf16[288,72]{0,1:T(8,128)(2,1)S(1)} %get-tuple-element.150), channel_id=1, source_target_pairs={{0,4},{2,6},{8,0},{10,2},{16,8},{18,10},{24,16},{26,18},{28,24},{3... | collective-permute-start | bytes 124424 | tf_op jit(solution)/shard_map/ppermute | solution.py:91
  10.6 136.7 %collective-permute-start.30 = (bf16[3,72,288]{2,1,0:T(8,128)(2,1)}, bf16[3,72,288]{2,1,0:T(8,128)(2,1)}, u32[]{:S(2)}, u32[]{:S(2)}) collective-permute-start(bf16[3,72,288]{2,1,0:T(8,128)(2,1)} %get-tuple-element.139), channel_id=1, source_target_pairs={{0,8},{2,10},{8,16},{10,18},{16,24},{18,26},{24,28},{26,30},{28,20... | collective-permute-start | bytes 373256 | tf_op jit(solution)/shard_map/ppermute | solution.py:90
  67.2 82.2 %collective-permute-start.37 = (bf16[3,72,288]{2,1,0:T(8,128)(2,1)}, bf16[3,72,288]{2,1,0:T(8,128)(2,1)}, u32[]{:S(2)}, u32[]{:S(2)}) collective-permute-start(bf16[3,72,288]{2,1,0:T(8,128)(2,1)} %get-tuple-element.140), channel_id=1, source_target_pairs={{0,4},{2,6},{8,0},{10,2},{16,8},{18,10},{24,16},{26,18},{28,24},{3... | collective-permute-start | bytes 373256 | tf_op jit(solution)/shard_map/ppermute | solution.py:91
  112.1 38.9 %collective-permute-start.61 = (bf16[72,1152]{1,0:T(8,128)(2,1)}, bf16[72,1152]{1,0:T(8,128)(2,1)}, u32[]{:S(2)}, u32[]{:S(2)}) collective-permute-start(bf16[72,1152]{1,0:T(8,128)(2,1)} %get-tuple-element.131), channel_id=1, source_target_pairs={{0,8},{2,10},{8,16},{10,18},{16,24},{18,26},{24,28},{26,30},{28,20... | collective-permute-start | bytes 497672 | tf_op jit(solution)/shard_map/ppermute | solution.py:90
  117.1 37.1 %collective-permute-start.68 = (bf16[72,1152]{1,0:T(8,128)(2,1)}, bf16[72,1152]{1,0:T(8,128)(2,1)}, u32[]{:S(2)}, u32[]{:S(2)}) collective-permute-start(bf16[72,1152]{1,0:T(8,128)(2,1)} %get-tuple-element.132), channel_id=1, source_target_pairs={{0,4},{2,6},{8,0},{10,2},{16,8},{18,10},{24,16},{26,18},{28,24},{3... | collective-permute-start | bytes 497672 | tf_op jit(solution)/shard_map/ppermute | solution.py:91
  149.4 129.2 %collective-permute-start.15 = (f32[8,4,6912]{2,1,0:T(4,128)}, f32[8,4,6912]{2,1,0:T(4,128)}, u32[]{:S(2)}, u32[]{:S(2)}) collective-permute-start(f32[8,4,6912]{2,1,0:T(4,128)} %select_bitcast_fusion), channel_id=1, source_target_pairs={{0,2},{2,0},{4,6},{6,4},{8,10},{10,8},{12,14},{14,12},{16,18},{18,... | collective-permute-start | bytes 2654216 | tf_op jit(solution)/shard_map/ppermute | solution.py:112
  198.0 71.5 %collective-permute-start.59 = (bf16[8,576,72]{1,2,0:T(8,128)(2,1)}, bf16[8,576,72]{1,2,0:T(8,128)(2,1)}, u32[]{:S(2)}, u32[]{:S(2)}) collective-permute-start(bf16[8,576,72]{1,2,0:T(8,128)(2,1)} %pad_maximum_fusion.13), channel_id=1, source_target_pairs={{0,2},{2,0},{4,6},{6,4},{8,10},{10,8},{12,14},{14,12},{16,18},{18,... | collective-permute-start | bytes 1990664 | tf_op jit(solution)/shard_map/ppermute | solution.py:98
  253.3 30.6 %collective-permute-start.73 = (bf16[72,1152]{1,0:T(8,128)(2,1)}, bf16[72,1152]{1,0:T(8,128)(2,1)S(1)}, u32[]{:S(2)}, u32[]{:S(2)}) collective-permute-start(bf16[72,1152]{1,0:T(8,128)(2,1)} %collective-permute-done.72), channel_id=1, source_target_pairs={{0,4},{2,6},{8,0},{10,2},{16,8},{18,10},{24,16},{26,18},{28,24},{3... | collective-permute-start | bytes 497672 | tf_op jit(solution)/shard_map/ppermute | solution.py:91
  278.6 76.5 %collective-permute-start.44 = (bf16[8,3,72,576]{3,2,1,0:T(8,128)(2,1)}, bf16[8,3,72,576]{3,2,1,0:T(8,128)(2,1)}, u32[]{:S(2)}, u32[]{:S(2)}) collective-permute-start(bf16[8,3,72,576]{3,2,1,0:T(8,128)(2,1)} %pad_maximum_fusion.9), channel_id=1, source_target_pairs={{0,2},{2,0},{4,6},{6,4},{8,10},{10,8},{12,14},{14,12},{16,18},{18,... | collective-permute-start | bytes 5971976 | tf_op jit(solution)/shard_map/ppermute | solution.py:98
  331.3 53.8 %collective-permute-start.90 = (bf16[8,2304,72]{1,2,0:T(8,128)(2,1)}, bf16[8,2304,72]{1,2,0:T(8,128)(2,1)}, u32[]{:S(2)}, u32[]{:S(2)}) collective-permute-start(bf16[8,2304,72]{1,2,0:T(8,128)(2,1)} %get-tuple-element.125), channel_id=1, source_target_pairs={{0,2},{2,0},{4,6},{6,4},{8,10},{10,8},{12,14},{14,12},{16,18},{18,... | collective-permute-start | bytes 7962632 | tf_op jit(solution)/shard_map/ppermute | solution.py:98
  334.4 62.8 %collective-permute-start.75 = (bf16[8,72,2304]{2,1,0:T(8,128)(2,1)}, bf16[8,72,2304]{2,1,0:T(8,128)(2,1)}, u32[]{:S(2)}, u32[]{:S(2)}) collective-permute-start(bf16[8,72,2304]{2,1,0:T(8,128)(2,1)} %get-tuple-element.123), channel_id=1, source_target_pairs={{0,2},{2,0},{4,6},{6,4},{8,10},{10,8},{12,14},{14,12},{16,18},{18,... | collective-permute-start | bytes 7962632 | tf_op jit(solution)/shard_map/ppermute | solution.py:98
  383.6 50.1 %collective-permute-start.60 = (f32[4,128,1152]{2,1,0:T(8,128)}, f32[4,128,1152]{2,1,0:T(8,128)}, u32[]{:S(2)}, u32[]{:S(2)}) collective-permute-start(f32[4,128,1152]{2,1,0:T(8,128)} %fusion.167), channel_id=1, source_target_pairs={{0,1},{1,0},{2,3},{3,2},{4,5},{5,4},{6,7},{7,6},{8,9},{9,8},{10,11... | collective-permute-start | bytes 7077896 | tf_op jit(solution)/shard_map/ppermute | solution.py:27
  445.0 48.9 %collective-permute-start.91 = (f32[4,128,1152]{2,1,0:T(8,128)S(1)}, f32[4,128,1152]{2,1,0:T(8,128)S(1)}, u32[]{:S(2)}, u32[]{:S(2)}) collective-permute-start(f32[4,128,1152]{2,1,0:T(8,128)S(1)} %fusion.150), channel_id=1, source_target_pairs={{0,1},{1,0},{2,3},{3,2},{4,5},{5,4},{6,7},{7,6},{8,9},{9,8},{10,11... | collective-permute-start | bytes 7077896 | tf_op jit(solution)/shard_map/ppermute | solution.py:27
  515.6 48.0 %collective-permute-start.92 = (f32[4,128,1152]{2,1,0:T(8,128)S(1)}, f32[4,128,1152]{2,1,0:T(8,128)S(1)}, u32[]{:S(2)}, u32[]{:S(2)}) collective-permute-start(f32[4,128,1152]{2,1,0:T(8,128)S(1)} %fusion.6), channel_id=1, source_target_pairs={{0,1},{1,0},{2,3},{3,2},{4,5},{5,4},{6,7},{7,6},{8,9},{9,8},{10,11... | collective-permute-start | bytes 7077896 | tf_op jit(solution)/shard_map/ppermute | solution.py:27
  528.6 178.3 %collective-permute-start.154 = (f32[8,2304,72]{1,2,0:T(8,128)}, f32[8,2304,72]{1,2,0:T(8,128)}, u32[]{:S(2)}, u32[]{:S(2)}) collective-permute-start(f32[8,2304,72]{1,2,0:T(8,128)} %fusion), channel_id=1, source_target_pairs={{0,2},{2,0},{4,6},{6,4},{8,10},{10,8},{12,14},{14,12},{16,18},{18,... | collective-permute-start | bytes 15925256 | tf_op jit(solution)/shard_map/ppermute | solution.py:112
  539.5 174.9 %collective-permute-start.139 = (f32[8,72,2304]{2,1,0:T(8,128)}, f32[8,72,2304]{2,1,0:T(8,128)}, u32[]{:S(2)}, u32[]{:S(2)}) collective-permute-start(f32[8,72,2304]{2,1,0:T(8,128)} %fusion.3), channel_id=1, source_target_pairs={{0,2},{2,0},{4,6},{6,4},{8,10},{10,8},{12,14},{14,12},{16,18},{18,... | collective-permute-start | bytes 15925256 | tf_op jit(solution)/shard_map/ppermute | solution.py:112
  592.0 54.0 %collective-permute-start.93 = (f32[4,128,1152]{2,1,0:T(8,128)}, f32[4,128,1152]{2,1,0:T(8,128)}, u32[]{:S(2)}, u32[]{:S(2)}) collective-permute-start(f32[4,128,1152]{2,1,0:T(8,128)} %convolution_bitcast_fusion.1), channel_id=1, source_target_pairs={{0,1},{1,0},{2,3},{3,2},{4,5},{5,4},{6,7},{7,6},{8,9},{9,8},{10,11... | collective-permute-start | bytes 7077896 | tf_op jit(solution)/shard_map/ppermute | solution.py:27
  631.1 31.2 %collective-permute-start.130 = (bf16[288,72]{0,1:T(8,128)(2,1)}, bf16[288,72]{0,1:T(8,128)(2,1)}, u32[]{:S(2)}, u32[]{:S(2)}) collective-permute-start(bf16[288,72]{0,1:T(8,128)(2,1)} %fusion.123), channel_id=1, source_target_pairs={{0,8},{2,10},{8,16},{10,18},{16,24},{18,26},{24,28},{26,30},{28,20... | collective-permute-start | bytes 124424 | tf_op jit(solution)/shard_map/ppermute | solution.py:120
  634.0 31.2 %collective-permute-start.138 = (bf16[288,72]{0,1:T(8,128)(2,1)}, bf16[288,72]{0,1:T(8,128)(2,1)}, u32[]{:S(2)}, u32[]{:S(2)}) collective-permute-start(bf16[288,72]{0,1:T(8,128)(2,1)} %fusion.116), channel_id=1, source_target_pairs={{0,4},{2,6},{8,0},{10,2},{16,8},{18,10},{24,16},{26,18},{28,24},{3... | collective-permute-start | bytes 124424 | tf_op jit(solution)/shard_map/ppermute | solution.py:120
  670.3 98.0 %collective-permute-start.109 = (f32[8,3,72,576]{3,2,1,0:T(8,128)}, f32[8,3,72,576]{3,2,1,0:T(8,128)}, u32[]{:S(2)}, u32[]{:S(2)}) collective-permute-start(f32[8,3,72,576]{3,2,1,0:T(8,128)} %fusion.19), channel_id=1, source_target_pairs={{0,2},{2,0},{4,6},{6,4},{8,10},{10,8},{12,14},{14,12},{16,18},{18,... | collective-permute-start | bytes 11943944 | tf_op jit(solution)/shard_map/ppermute | solution.py:112
  706.7 84.3 %collective-permute-start.108 = (f32[8,40320]{1,0:T(8,128)}, f32[8,40320]{1,0:T(8,128)}, u32[]{:S(2)}, u32[]{:S(2)}) collective-permute-start(f32[8,40320]{1,0:T(8,128)} %pad_maximum_fusion.12), channel_id=1, source_target_pairs={{0,2},{2,0},{4,6},{6,4},{8,10},{10,8},{12,14},{14,12},{16,18},{18,... | collective-permute-start | bytes 3870728 | tf_op jit(solution)/shard_map/ppermute | solution.py:98
  (260 other events, 4172.7 us)

commit v3 on v2

--- a/solution.py
+++ b/solution.py
@@ -71,6 +71,8 @@
         self.forward = step(1)
         self.backward = step(-1)
         self.swap = [(2 * k + c, 2 * k + 1 - c) for k in range(self.n) for c in range(2)]
+        n_dp = 2 * self.n
+        self.bits = n_dp.bit_length() - 1 if n_dp & (n_dp - 1) == 0 else None
 
     def place(self):
         index = lax.axis_index("dp")
@@ -79,12 +81,13 @@
         p = jnp.asarray(self.position, jnp.int32)[chip]
         return chip, core, p
 
-    def gather(self, shard, split_axis):
+    def gather(self, shards):
         if self.native:
-            return lax.all_gather(shard, "dp", axis=0, tiled=False)
+            return [lax.all_gather(s, "dp", axis=0, tiled=False) for s in shards]
         n = self.n
         chip, core, p = self.place()
-        a, b = jnp.split(shard, 2, axis=split_axis)
+        flat = jnp.concatenate([s.reshape(-1) for s in shards])
+        a, b = jnp.split(flat, 2)
         got_a, got_b = [a], [b]
         for _ in range(1, n):
             a = lax.ppermute(a, "dp", self.forward)
@@ -94,23 +97,32 @@
         positions = jnp.asarray(self.position, jnp.int32)
         from_a = jnp.take(jnp.stack(got_a), (p - positions) % n, axis=0)
         from_b = jnp.take(jnp.stack(got_b), (positions - p) % n, axis=0)
-        mine = jnp.concatenate([from_a, from_b], axis=split_axis + 1)
+        mine = jnp.concatenate([from_a, from_b], axis=1)
         other = lax.ppermute(mine, "dp", self.swap)
         pair = jnp.stack([mine, other], axis=1)
-        pair = jnp.take(pair, jnp.stack([core, 1 - core]), axis=1)
-        return pair.reshape((2 * n,) + shard.shape)
-
-    def reduce(self, blocks, split_axis, wire):
+        pair = jnp.take(pair, jnp.stack([core, 1 - core]), axis=1).reshape(2 * n, -1)
+        out = []
+        offset = 0
+        for s in shards:
+            out.append(pair[:, offset : offset + s.size].reshape((2 * n,) + s.shape))
+            offset += s.size
+        return out
+
+    def reduce(self, block_sets, wire):
         if self.native:
-            return lax.psum_scatter(blocks, "dp", scatter_dimension=0, tiled=False)
+            return [lax.psum_scatter(b, "dp", scatter_dimension=0, tiled=False) for b in block_sets]
         n = self.n
         chip, core, p = self.place()
         order = jnp.asarray(self.order, jnp.int32)
-        paired = blocks.reshape((n, 2) + blocks.shape[1:])
-        mine = jnp.take(paired, core, axis=1)
-        theirs = jnp.take(paired, 1 - core, axis=1)
-        summed = mine + lax.ppermute(theirs, "dp", self.swap)
-        half_a, half_b = jnp.split(summed, 2, axis=split_axis + 1)
+        mines, theirs = [], []
+        for blocks in block_sets:
+            paired = blocks.reshape(n, 2, -1)
+            mines.append(jnp.take(paired, core, axis=1))
+            theirs.append(jnp.take(paired, 1 - core, axis=1))
+        summed = jnp.concatenate(mines, axis=1) + lax.ppermute(
+            jnp.concatenate(theirs, axis=1), "dp", self.swap
+        )
+        half_a, half_b = jnp.split(summed, 2, axis=1)
         results = []
         for half, perm, sign in ((half_a, self.forward, 1), (half_b, self.backward, -1)):
             carried = None
@@ -120,7 +132,41 @@
                 carried = lax.ppermute(total.astype(wire), "dp", perm).astype(jnp.float32)
             own = lax.dynamic_index_in_dim(half, chip, axis=0, keepdims=False)
             results.append(carried + own)
-        return jnp.concatenate(results, axis=split_axis)
+        flat = jnp.concatenate(results)
+        out = []
+        offset = 0
+        for blocks in block_sets:
+            size = blocks[0].size
+            out.append(flat[offset : offset + size].reshape(blocks.shape[1:]))
+            offset += size
+        return out
+
+    def small_gather(self, shard):
+        if self.native or self.bits is None:
+            return lax.all_gather(shard, "dp", axis=0, tiled=False)
+        index = lax.axis_index("dp")
+        held = shard[None]
+        for bit in range(self.bits):
+            partner = [(d, d ^ (1 << bit)) for d in range(2 * self.n)]
+            other = lax.ppermute(held, "dp", partner)
+            low = (index >> bit) % 2 == 0
+            held = jnp.where(low, jnp.concatenate([held, other]), jnp.concatenate([other, held]))
+        return held
+
+    def small_reduce(self, blocks):
+        if self.native or self.bits is None:
+            return lax.psum_scatter(blocks, "dp", scatter_dimension=0, tiled=False)
+        index = lax.axis_index("dp")
+        held = blocks
+        for bit in reversed(range(self.bits)):
+            partner = [(d, d ^ (1 << bit)) for d in range(2 * self.n)]
+            half = held.shape[0] // 2
+            low_part, high_part = held[:half], held[half:]
+            low = (index >> bit) % 2 == 0
+            keep = jnp.where(low, low_part, high_part)
+            give = jnp.where(low, high_part, low_part)
+            held = keep + lax.ppermute(give, "dp", partner)
+        return held[0]
 
 
 def attention_scores(query, key_rows, keymask, scale_factor):
@@ -164,10 +210,9 @@
     keymask = jnp.arange(keep)[None, :] < valid[:, None]
     rowmask = keymask[:, :, None]
 
-    incoming_weight = ring.gather(input_weight, 2)
-    outgoing_weight = ring.gather(output_weight, 0)
-    expert_weight_rows = ring.gather(expand_weight, 1).reshape(width, -1)
-    narrowing_weight = ring.gather(shrink_weight, 0)
+    incoming_weight, outgoing_weight = ring.gather([input_weight, output_weight])
+    expert_weight_rows, narrowing_weight = ring.gather([expand_weight, shrink_weight])
+    expert_weight_rows = expert_weight_rows.reshape(width, -1)
     inner = incoming_weight.shape[3]
     heads_here = inner // HEAD_DIM
     qv_bias = query_value_bias.astype(f32)
@@ -176,10 +221,10 @@
     narrowing_bias = shrink_bias.astype(f32)
 
     silu_cond = jax.nn.silu(conditioning.astype(f32)).astype(bf16)
-    silu_all = ring.gather(silu_cond, 1).reshape(-1, width)
+    silu_all = ring.small_gather(silu_cond).reshape(-1, width)
     silu_cols = lax.dynamic_slice_in_dim(silu_all, dp_index * d_shard, d_shard, axis=1)
     mod_partial = jnp.dot(silu_cols, modulation_weight, preferred_element_type=f32)
-    modulation = ring.reduce(mod_partial.reshape(n_dp, batch, -1), 1, f32)
+    modulation = ring.small_reduce(mod_partial.reshape(n_dp, batch, -1))
     modulation = modulation + modulation_bias.astype(f32)
     pieces = modulation.reshape(batch, 6, 1, width)
     shift_one, scale_one, gate_one = (pieces[:, 0], pieces[:, 1], pieces[:, 2])
@@ -249,7 +294,6 @@
     narrowing_term = jnp.einsum(
         "bku,bkdr->dur", activation_reduced, blocks(perceptron_gradient_reduced), preferred_element_type=f32
     )
-    shrink_weight_grad = ring.reduce(narrowing_term, 0, bf16)
     (grad_pre,) = pull_act(
         jnp.einsum(
             "bkdr,dur->bku", blocks(perceptron_gradient_reduced), narrowing_weight, preferred_element_type=f32
@@ -259,7 +303,9 @@
     widening_term = jnp.einsum(
         "cnq,cne->qe", second_reduced, preactivation_gradient_reduced, preferred_element_type=f32
     )
-    expand_weight_grad = ring.reduce(widening_term.reshape(n_dp, d_shard, -1), 1, bf16)
+    expand_weight_grad, shrink_weight_grad = ring.reduce(
+        [widening_term.reshape(n_dp, d_shard, -1), narrowing_term], bf16
+    )
     grad_second = model_sum(
         jnp.einsum(
             "pem,sm->pes", preactivation_gradient_reduced, expert_weight_rows, preferred_element_type=f32
@@ -273,7 +319,6 @@
     output_summand = jnp.einsum(
         "bkh,bkdr->dhr", attention_result, blocks(attention_gradient_reduced), preferred_element_type=f32
     )
-    output_weight_grad = ring.reduce(output_summand, 0, bf16)
     grad_attended = (
         jnp.einsum(
             "bkdr,dhr->bkh", blocks(attention_gradient_reduced), outgoing_weight, preferred_element_type=f32
@@ -301,7 +346,7 @@
     input_summand = jnp.einsum(
         "bkdr,lbku->dlru", blocks(first_reduced), projection_gradient_reduced, preferred_element_type=f32
     )
-    input_weight_grad = ring.reduce(input_summand, 2, bf16)
+    input_weight_grad, output_weight_grad = ring.reduce([input_summand, output_summand], bf16)
     grad_first = model_sum(
         jnp.einsum(
             "lbku,dlru->bkdr", projection_gradient_reduced, incoming_weight, preferred_element_type=f32
@@ -325,7 +370,7 @@
         jnp.sum(grad_pre, axis=(0, 1)),
         jnp.sum(grad_mlp, axis=(0, 1)),
     )
-    gathered = ring.gather(jnp.concatenate((grad_mod.reshape(-1),) + bias_terms), 0)
+    gathered = ring.small_gather(jnp.concatenate((grad_mod.reshape(-1),) + bias_terms))
     grad_mod_all = gathered[:, : grad_mod.size].reshape(-1, 6 * width).astype(bf16)
     modulation_weight_grad = jnp.einsum(
         "bd,be->de", silu_cols, grad_mod_all, preferred_element_type=f32

time: 860 us -> 1190 us (1.38)
  local copies, waits for them, and re-layouts: 201 us -> 511 us
  starting transfers between devices: 190 us -> 119 us
  other arithmetic: 126 us -> 190 us
  matrix products: 75.7 us -> 90.7 us
    reshape x0 -> x12, local copies, waits for them, and re-layouts: none -> 93.2 us  [the longest x3 45 us: reduce(): paired = blocks.reshape(n, 2, -1)]
    ppermute x5 -> x14, waiting for transfers between devices: 0.01 us -> 77.5 us  [the longest x8 74.3 us: small_gather(): other = lax.ppermute(held, 'dp', partner)]
    ppermute x70 -> x28, starting transfers between devices: 76.8 us -> 29.5 us  [reduce(): carried = lax.ppermute(total.astype(wire), 'dp', perm).astype(jnp.float32)]
    another operation x14 -> x18, local copies, waits for them, and re-layouts: 7.75 us -> 50.2 us  [gather(): from_b = jnp.take(jnp.stack(got_b), (positions - p) % n, axis=0)]
    another operation x14 -> x17, local copies, waits for them, and re-layouts: 5.7 us -> 46.6 us  [gather(): from_a = jnp.take(jnp.stack(got_a), (p - positions) % n, axis=0)]
    dynamic_slice x0 -> x2, local copies, waits for them, and re-layouts: none -> 38.2 us  [reduce(): lax.dynamic_index_in_dim(half, order[(p - sign * t) % n], axis=0, keepdim...]
    another operation x2 -> x4, local copies, waits for them, and re-layouts: 5.53 us -> 37.6 us  [the longest x2 19.4 us: reduce(): mines.append(jnp.take(paired, core, axis=1))]
    ppermute x42 -> x14, starting transfers between devices: 36.7 us -> 9.49 us  [gather(): b = lax.ppermute(b, 'dp', self.backward)]
  transfers between devices with their start and end apart: 169 -> 76, of which waited for: 89 -> 35; matrix products, arithmetic and copies ran while one was open for 41% -> 49% of each run, Pallas kernels for 0% -> 0%
where the time goes in v3:
time: 1190 us; the launch traced here: 1170 us
  local copies, waits for them, and re-layouts  511 us (43%)
  waiting for transfers between devices  221 us (19%)
  other arithmetic  190 us (16%)
  starting transfers between devices  119 us (10%)
  matrix products  90.7 us (8%)
  between operations  39.3 us (3%)
    ppermute x8, waiting for transfers between devices, small_gather(): other = lax.ppermute(held, 'dp', partner)  74.3 us
    unnamed x242, local copies, waits for them, and re-layouts  68.2 us
    ppermute x28, waiting for transfers between devices, reduce(): carried = lax.ppermute(total.astype(wire), 'dp', perm).astype(jnp.float32)  64.8 us
    ppermute x4, waiting for transfers between devices, model_sum(): other = lax.ppermute(partial, 'mp', [(0, 1), (1, 0)])  64.6 us
    ppermute x14, starting transfers between devices, gather(): a = lax.ppermute(a, 'dp', self.forward)  56.8 us
    another operation x18, local copies, waits for them, and re-layouts, gather(): from_b = jnp.take(jnp.stack(got_b), (positions - p) % n, axis=0)  50.2 us
    another operation x17, local copies, waits for them, and re-layouts, gather(): from_a = jnp.take(jnp.stack(got_a), (p - positions) % n, axis=0)  46.6 us
    reshape x3, local copies, waits for them, and re-layouts, reduce(): paired = blocks.reshape(n, 2, -1)  45 us
  transfers between devices with their start and end apart: 76, of which 35 were waited for; matrix products, arithmetic and copies ran while one was open for 49% of the time, Pallas kernels for 0%

profile of v3, /device:TPU:0, one launch (start us, length us, event | category | flops | bytes accessed | tf_op | source)
XLA Modules:
  0.0 1170.5 jit_solution(5320049159729991516)
XLA Ops:
  54.9 17.5 %collective-permute-start.25 = (bf16[165888]{0:T(1024)(128)(2,1)}, bf16[165888]{0:T(1024)(128)(2,1)}, u32[]{:S(2)}, u32[]{:S(2)}) collective-permute-start(bf16[165888]{0:T(1024)(128)(2,1)} %collective-permute-done.24), channel_id=1, source_target_pairs={{0,8},{2,10},{8,16},{10,18},{16,24},{18,26},{24,28},{26,30},{28,20... | collective-permute-start | bytes 995336 | tf_op jit(solution)/shard_map/ppermute | solution.py:93
  76.1 17.0 %collective-permute-start.11 = (bf16[82944]{0:T(1024)(128)(2,1)S(1)}, bf16[82944]{0:T(1024)(128)(2,1)S(1)}, u32[]{:S(2)}, u32[]{:S(2)}) collective-permute-start(bf16[82944]{0:T(1024)(128)(2,1)S(1)} %collective-permute-done.10), channel_id=1, source_target_pairs={{0,8},{2,10},{8,16},{10,18},{16,24},{18,26},{24,28},{26,30},{28,20... | collective-permute-start | bytes 497672 | tf_op jit(solution)/shard_map/ppermute | solution.py:93
  200.5 10.8 fusion.89
  238.2 14.9 %stack.192 = bf16[8,165888]{1,0:T(8,128)(2,1)} concatenate(bf16[1,165888]{1,0:T(2,128)(2,1)S(1)} %copy-done.56, bf16[1,165888]{1,0:T(2,128)(2,1)} %stack.185, bf16[1,165888]{1,0:T(2,128)(2,1)} %stack.186, bf16[1,165888]{1,0:T(2,128)(2,1)} %stack.187, bf16[1,165888]{1,0:T(2,128)(2,1)} %stack.188, bf16[1,165888]{1,0:T(2,128)(2,1)} %stack.189, bf16[1,165888]{1,0:T(2,128)(2,1)} %stack.190, ...), dimensions={0} | concatenate | bytes 5308416 | tf_op jit(solution)/shard_map/stack | solution.py:99
  267.8 14.9 %stack.184 = bf16[8,165888]{1,0:T(8,128)(2,1)} concatenate(bf16[1,165888]{1,0:T(2,128)(2,1)S(1)} %bitcast.295, bf16[1,165888]{1,0:T(2,128)(2,1)} %stack.177, bf16[1,165888]{1,0:T(2,128)(2,1)} %stack.178, bf16[1,165888]{1,0:T(2,128)(2,1)} %stack.179, bf16[1,165888]{1,0:T(2,128)(2,1)} %stack.180, bf16[1,165888]{1,0:T(2,128)(2,1)} %stack.181, bf16[1,165888]{1,0:T(2,128)(2,1)} %stack.182, ...), dimensions={0} | concatenate | bytes 5308416 | tf_op jit(solution)/shard_map/stack | solution.py:98
  309.5 20.3 %fusion.91 = (bf16[8,1,331776]{2,0,1:T(8,128)(2,1)}, bf16[8,331776]{1,0:T(8,128)(2,1)}) fusion(bf16[8,165888]{1,0:T(8,128)(2,1)S(1)} %maximum_select_fusion.1, bf16[8,165888]{1,0:T(8,128)(2,1)S(1)} %maximum_select_fusion), kind=kLoop, calls=%fused_computation.308 | loop fusion | flops 10616832 | bytes 15925248 | tf_op jit(solution)/shard_map/stack | solution.py:102
  346.5 13.5 %copy.139 = bf16[8,2,165888]{2,1,0:T(2,128)(2,1)} copy(bf16[8,2,165888]{2,0,1:T(8,128)(2,1)S(1)} %pad_maximum_fusion.2) | data formatting | bytes 10616832
  408.9 52.1 %collective-permute-done.23 = f32[4,128,1152]{2,1,0:T(8,128)S(1)} collective-permute-done((f32[4,128,1152]{2,1,0:T(8,128)S(1)}, f32[4,128,1152]{2,1,0:T(8,128)S(1)}, u32[]{:S(2)}, u32[]{:S(2)}) %collective-permute-start.23) | collective-permute-done | bytes 2359328 | tf_op jit(solution)/shard_map/ppermute | solution.py:27
  485.5 9.8 pad_maximum_fusion
  495.4 28.9 %copy.147 = bf16[8,2,331776]{2,1,0:T(2,128)(2,1)} copy(bf16[8,2,331776]{2,0,1:T(8,128)(2,1)S(1)} %pad_maximum_fusion) | data formatting | bytes 21233664
  524.3 13.7 %gather.30 = bf16[16,331776]{1,0:T(8,128)(2,1)} reshape(bf16[8,2,331776]{2,1,0:T(2,128)(2,1)} %copy.147) | data formatting | bytes 21233664 | tf_op jit(solution)/shard_map/jit(_take)/gather | solution.py:103
  553.8 28.1 %reshape.481 = bf16[16,2304,72]{2,1,0:T(8,128)(2,1)} reshape(bf16[16,165888]{1,0:T(8,128)(2,1)} %get-tuple-element.119) | data formatting | bytes 10616832 | tf_op jit(solution)/shard_map/reshape | solution.py:107
  581.9 11.3 copy.148
  665.5 11.9 %fusion.102 = (f32[2304]{0:T(1024)S(1)}, bf16[4,128,2304]{2,1,0:T(8,128)(2,1)S(1)}) fusion(f32[4,128,2304]{2,1,0:T(8,128)} %copy-done.107, bf16[4,128,16,72]{1,3,2,0:T(8,128)(2,1)} %bitcast.316, bf16[16,2304,72]{2,1,0:T(8,128)(2,1)} %reshape.481), kind=kOutput, calls=%fused_computation.319 | convolution fusion | flops 2742679296 | bytes 13575168 | tf_op jit(solution)/shard_map/bkdr,dur->bku/dot_general | solution.py:298
  701.1 12.6 %reshape_reshape.11 = f32[8,2,165888]{2,1,0:T(2,128)} reshape(f32[1152,2304]{1,0:T(8,128)} %convolution_bitcast_fusion) | data formatting | bytes 21233664 | tf_op jit(solution)/shard_map/reshape;reshape | solution.py:119
  713.7 14.0 %constant_dynamic-slice_fusion.2 = (f32[8,1,165888]{2,1,0:T(1,128)}, f32[8,1,165888]{2,1,0:T(1,128)}) fusion(f32[8,2,165888]{2,1,0:T(2,128)} %reshape_reshape.11, s32[]{:T(128)S(6)} %select_n.756, s32[]{:T(128)S(6)} %select_n.760), kind=kLoop, calls=%fused_computation.229 | loop fusion | bytes 21233672 | tf_op jit(solution)/shard_map/jit(_take) | solution.py:120
  727.7 15.2 %copy.171 = f32[16,2304,72]{2,1,0:T(8,128)} copy(f32[16,2304,72]{1,2,0:T(8,128)} %convolution_bitcast_fusion.1) | data formatting | bytes 21233664 | tf_op jit(solution)/shard_map/bku,bkdr->dur/transpose | solution.py:294
  742.9 25.0 %reshape.493 = f32[8,2,165888]{2,1,0:T(2,128)} reshape(f32[16,2304,72]{2,1,0:T(8,128)} %copy.171) | data formatting | bytes 21233664 | tf_op jit(solution)/shard_map/reshape | solution.py:119
  773.5 10.9 constant_dynamic-slice_fusion.5
  841.8 12.2 %reshape.490 = f32[8,2,124416]{2,1,0:T(2,128)} reshape(f32[16,3,72,576]{3,2,1,0:T(8,128)} %copy.164) | data formatting | bytes 15925248 | tf_op jit(solution)/shard_map/reshape | solution.py:119
  854.0 11.2 constant_dynamic-slice_fusion.3
  914.4 11.8 %collective-permute-done.44 = f32[4,40320]{1,0:T(4,128)S(1)} collective-permute-done((f32[4,40320]{1,0:T(4,128)S(1)}, f32[4,40320]{1,0:T(4,128)S(1)}, u32[]{:S(2)}, u32[]{:S(2)}) %collective-permute-start.44) | collective-permute-done | bytes 645152 | tf_op jit(solution)/shard_map/ppermute | solution.py:151
  932.5 51.8 %collective-permute-done.45 = f32[8,40320]{1,0:T(8,128)S(1)} collective-permute-done((f32[8,40320]{1,0:T(8,128)S(1)}, f32[8,40320]{1,0:T(8,128)S(1)}, u32[]{:S(2)}, u32[]{:S(2)}) %collective-permute-start.45) | collective-permute-done | bytes 1290272 | tf_op jit(solution)/shard_map/ppermute | solution.py:151
  1065.7 35.0 %constant_dynamic-slice_fusion.7 = (f32[1,165888]{1,0:T(1,128)}, f32[1,165888]{1,0:T(1,128)S(1)}, f32[1,165888]{1,0:T(1,128)S(1)}, f32[1,165888]{1,0:T(1,128)}, ...) fusion(f32[8,165888]{1,0:T(8,128)} %get-tuple-element.112, ...), kind=kLoop, calls=%fused_computation.234 | loop fusion | bytes 18579508 | tf_op jit(solution)/shard_map/jit(dynamic_index_in_dim)/dynamic_slice | solution.py:130
  (632 shorter events, 666.8 us)
Async XLA Ops:
  3.9 40.1 %collective-permute-start.8 = (bf16[82944]{0:T(1024)(128)(2,1)}, bf16[82944]{0:T(1024)(128)(2,1)}, u32[]{:S(2)}, u32[]{:S(2)}) collective-permute-start(bf16[82944]{0:T(1024)(128)(2,1)} %split.21), channel_id=1, source_target_pairs={{0,8},{2,10},{8,16},{10,18},{16,24},{18,26},{24,28},{26,30},{28,20... | collective-permute-start | bytes 497672 | tf_op jit(solution)/shard_map/ppermute | solution.py:93
  9.8 36.1 %collective-permute-start.15 = (bf16[82944]{0:T(1024)(128)(2,1)}, bf16[82944]{0:T(1024)(128)(2,1)}, u32[]{:S(2)}, u32[]{:S(2)}) collective-permute-start(bf16[82944]{0:T(1024)(128)(2,1)} %pad_maximum_fusion.10), channel_id=1, source_target_pairs={{0,4},{2,6},{8,0},{10,2},{16,8},{18,10},{24,16},{26,18},{28,24},{3... | collective-permute-start | bytes 497672 | tf_op jit(solution)/shard_map/ppermute | solution.py:94
  10.9 44.0 %collective-permute-start.24 = (bf16[165888]{0:T(1024)(128)(2,1)}, bf16[165888]{0:T(1024)(128)(2,1)}, u32[]{:S(2)}, u32[]{:S(2)}) collective-permute-start(bf16[165888]{0:T(1024)(128)(2,1)} %reshape.479), channel_id=1, source_target_pairs={{0,8},{2,10},{8,16},{10,18},{16,24},{18,26},{24,28},{26,30},{28,20... | collective-permute-start | bytes 995336 | tf_op jit(solution)/shard_map/ppermute | solution.py:93
  15.1 57.3 %collective-permute-start.31 = (bf16[165888]{0:T(1024)(128)(2,1)}, bf16[165888]{0:T(1024)(128)(2,1)}, u32[]{:S(2)}, u32[]{:S(2)}) collective-permute-start(bf16[165888]{0:T(1024)(128)(2,1)} %reshape.480), channel_id=1, source_target_pairs={{0,4},{2,6},{8,0},{10,2},{16,8},{18,10},{24,16},{26,18},{28,24},{3... | collective-permute-start | bytes 995336 | tf_op jit(solution)/shard_map/ppermute | solution.py:94
  49.8 106.3 %collective-permute-start.4 = (f32[8,4,6912]{2,1,0:T(4,128)}, f32[8,4,6912]{2,1,0:T(4,128)}, u32[]{:S(2)}, u32[]{:S(2)}) collective-permute-start(f32[8,4,6912]{2,1,0:T(4,128)} %select_n.603), channel_id=1, source_target_pairs={{0,16},{2,18},{4,20},{6,22},{8,24},{10,26},{12,28},{14,30},{16,0},... | collective-permute-start | bytes 2654216 | tf_op jit(solution)/shard_map/ppermute | solution.py:168
  54.9 38.2 %collective-permute-start.17 = (bf16[82944]{0:T(1024)(128)(2,1)}, bf16[82944]{0:T(1024)(128)(2,1)S(1)}, u32[]{:S(2)}, u32[]{:S(2)}) collective-permute-start(bf16[82944]{0:T(1024)(128)(2,1)} %collective-permute-done.16), channel_id=1, source_target_pairs={{0,4},{2,6},{8,0},{10,2},{16,8},{18,10},{24,16},{26,18},{28,24},{3... | collective-permute-start | bytes 497672 | tf_op jit(solution)/shard_map/ppermute | solution.py:94
  54.9 48.0 %collective-permute-start.25 = (bf16[165888]{0:T(1024)(128)(2,1)}, bf16[165888]{0:T(1024)(128)(2,1)}, u32[]{:S(2)}, u32[]{:S(2)}) collective-permute-start(bf16[165888]{0:T(1024)(128)(2,1)} %collective-permute-done.24), channel_id=1, source_target_pairs={{0,8},{2,10},{8,16},{10,18},{16,24},{18,26},{24,28},{26,30},{28,20... | collective-permute-start | bytes 995336 | tf_op jit(solution)/shard_map/ppermute | solution.py:93
  72.4 33.1 %collective-permute-start.32 = (bf16[165888]{0:T(1024)(128)(2,1)}, bf16[165888]{0:T(1024)(128)(2,1)}, u32[]{:S(2)}, u32[]{:S(2)}) collective-permute-start(bf16[165888]{0:T(1024)(128)(2,1)} %collective-permute-done.31), channel_id=1, source_target_pairs={{0,4},{2,6},{8,0},{10,2},{16,8},{18,10},{24,16},{26,18},{28,24},{3... | collective-permute-start | bytes 995336 | tf_op jit(solution)/shard_map/ppermute | solution.py:94
  102.9 50.5 %collective-permute-start.26 = (bf16[165888]{0:T(1024)(128)(2,1)}, bf16[165888]{0:T(1024)(128)(2,1)}, u32[]{:S(2)}, u32[]{:S(2)}) collective-permute-start(bf16[165888]{0:T(1024)(128)(2,1)} %collective-permute-done.25), channel_id=1, source_target_pairs={{0,8},{2,10},{8,16},{10,18},{16,24},{18,26},{24,28},{26,30},{28,20... | collective-permute-start | bytes 995336 | tf_op jit(solution)/shard_map/ppermute | solution.py:93
  105.5 44.0 %collective-permute-start.33 = (bf16[165888]{0:T(1024)(128)(2,1)}, bf16[165888]{0:T(1024)(128)(2,1)}, u32[]{:S(2)}, u32[]{:S(2)}) collective-permute-start(bf16[165888]{0:T(1024)(128)(2,1)} %collective-permute-done.32), channel_id=1, source_target_pairs={{0,4},{2,6},{8,0},{10,2},{16,8},{18,10},{24,16},{26,18},{28,24},{3... | collective-permute-start | bytes 995336 | tf_op jit(solution)/shard_map/ppermute | solution.py:94
  107.5 40.0 %collective-permute-start.13 = (bf16[82944]{0:T(1024)(128)(2,1)}, bf16[82944]{0:T(1024)(128)(2,1)}, u32[]{:S(2)}, u32[]{:S(2)}) collective-permute-start(bf16[82944]{0:T(1024)(128)(2,1)} %collective-permute-done.12), channel_id=1, source_target_pairs={{0,8},{2,10},{8,16},{10,18},{16,24},{18,26},{24,28},{26,30},{28,20... | collective-permute-start | bytes 497672 | tf_op jit(solution)/shard_map/ppermute | solution.py:93
  149.4 45.6 %collective-permute-start.34 = (bf16[165888]{0:T(1024)(128)(2,1)}, bf16[165888]{0:T(1024)(128)(2,1)}, u32[]{:S(2)}, u32[]{:S(2)}) collective-permute-start(bf16[165888]{0:T(1024)(128)(2,1)} %collective-permute-done.33), channel_id=1, source_target_pairs={{0,4},{2,6},{8,0},{10,2},{16,8},{18,10},{24,16},{26,18},{28,24},{3... | collective-permute-start | bytes 995336 | tf_op jit(solution)/shard_map/ppermute | solution.py:94
  153.5 41.3 %collective-permute-start.27 = (bf16[165888]{0:T(1024)(128)(2,1)}, bf16[165888]{0:T(1024)(128)(2,1)}, u32[]{:S(2)}, u32[]{:S(2)}) collective-permute-start(bf16[165888]{0:T(1024)(128)(2,1)} %collective-permute-done.26), channel_id=1, source_target_pairs={{0,8},{2,10},{8,16},{10,18},{16,24},{18,26},{24,28},{26,30},{28,20... | collective-permute-start | bytes 995336 | tf_op jit(solution)/shard_map/ppermute | solution.py:93
  211.3 118.5 %collective-permute-start.22 = (bf16[8,165888]{1,0:T(8,128)(2,1)}, bf16[8,165888]{1,0:T(8,128)(2,1)}, u32[]{:S(2)}, u32[]{:S(2)}) collective-permute-start(bf16[8,165888]{1,0:T(8,128)(2,1)} %get-tuple-element.168), channel_id=1, source_target_pairs={{0,2},{2,0},{4,6},{6,4},{8,10},{10,8},{12,14},{14,12},{16,18},{18,... | collective-permute-start | bytes 7962632 | tf_op jit(solution)/shard_map/ppermute | solution.py:101
  233.2 33.5 %collective-permute-start.30 = (bf16[165888]{0:T(1024)(128)(2,1)}, bf16[165888]{0:T(1024)(128)(2,1)S(1)}, u32[]{:S(2)}, u32[]{:S(2)}) collective-permute-start(bf16[165888]{0:T(1024)(128)(2,1)} %collective-permute-done.29), channel_id=1, source_target_pairs={{0,8},{2,10},{8,16},{10,18},{16,24},{18,26},{24,28},{26,30},{28,20... | collective-permute-start | bytes 995336 | tf_op jit(solution)/shard_map/ppermute | solution.py:93
  329.8 133.0 %collective-permute-start.38 = (bf16[8,331776]{1,0:T(8,128)(2,1)}, bf16[8,331776]{1,0:T(8,128)(2,1)}, u32[]{:S(2)}, u32[]{:S(2)}) collective-permute-start(bf16[8,331776]{1,0:T(8,128)(2,1)} %get-tuple-element.142), channel_id=1, source_target_pairs={{0,2},{2,0},{4,6},{6,4},{8,10},{10,8},{12,14},{14,12},{16,18},{18,... | collective-permute-start | bytes 15925256 | tf_op jit(solution)/shard_map/ppermute | solution.py:101
  407.3 53.7 %collective-permute-start.23 = (f32[4,128,1152]{2,1,0:T(8,128)S(1)}, f32[4,128,1152]{2,1,0:T(8,128)S(1)}, u32[]{:S(2)}, u32[]{:S(2)}) collective-permute-start(f32[4,128,1152]{2,1,0:T(8,128)S(1)} %fusion.103), channel_id=1, source_target_pairs={{0,1},{1,0},{2,3},{3,2},{4,5},{5,4},{6,7},{7,6},{8,9},{9,8},{10,11... | collective-permute-start | bytes 7077896 | tf_op jit(solution)/shard_map/ppermute | solution.py:27
  604.8 53.2 %collective-permute-start.39 = (f32[4,128,1152]{2,1,0:T(8,128)}, f32[4,128,1152]{2,1,0:T(8,128)}, u32[]{:S(2)}, u32[]{:S(2)}) collective-permute-start(f32[4,128,1152]{2,1,0:T(8,128)} %fusion.90), channel_id=1, source_target_pairs={{0,1},{1,0},{2,3},{3,2},{4,5},{5,4},{6,7},{7,6},{8,9},{9,8},{10,11... | collective-permute-start | bytes 7077896 | tf_op jit(solution)/shard_map/ppermute | solution.py:27
  699.6 109.7 %collective-permute-start.40 = (f32[4,128,1152]{2,1,0:T(8,128)}, f32[4,128,1152]{2,1,0:T(8,128)}, u32[]{:S(2)}, u32[]{:S(2)}) collective-permute-start(f32[4,128,1152]{2,1,0:T(8,128)} %fusion.51), channel_id=1, source_target_pairs={{0,1},{1,0},{2,3},{3,2},{4,5},{5,4},{6,7},{7,6},{8,9},{9,8},{10,11... | collective-permute-start | bytes 7077896 | tf_op jit(solution)/shard_map/ppermute | solution.py:27
  804.0 240.5 %collective-permute-start.61 = (f32[8,331776]{1,0:T(8,128)}, f32[8,331776]{1,0:T(8,128)}, u32[]{:S(2)}, u32[]{:S(2)}) collective-permute-start(f32[8,331776]{1,0:T(8,128)} %pad_maximum_fusion.1), channel_id=1, source_target_pairs={{0,2},{2,0},{4,6},{6,4},{8,10},{10,8},{12,14},{14,12},{16,18},{18,... | collective-permute-start | bytes 31850504 | tf_op jit(solution)/shard_map/ppermute | solution.py:122
  834.6 53.9 %collective-permute-start.41 = (f32[4,128,1152]{2,1,0:T(8,128)}, f32[4,128,1152]{2,1,0:T(8,128)}, u32[]{:S(2)}, u32[]{:S(2)}) collective-permute-start(f32[4,128,1152]{2,1,0:T(8,128)} %convolution_bitcast_fusion.3), channel_id=1, source_target_pairs={{0,1},{1,0},{2,3},{3,2},{4,5},{5,4},{6,7},{7,6},{8,9},{9,8},{10,11... | collective-permute-start | bytes 7077896 | tf_op jit(solution)/shard_map/ppermute | solution.py:27
  926.7 57.7 %collective-permute-start.45 = (f32[8,40320]{1,0:T(8,128)S(1)}, f32[8,40320]{1,0:T(8,128)S(1)}, u32[]{:S(2)}, u32[]{:S(2)}) collective-permute-start(f32[8,40320]{1,0:T(8,128)S(1)} %maximum_select_fusion.3), channel_id=1, source_target_pairs={{0,16},{2,18},{4,20},{6,22},{8,24},{10,26},{12,28},{14,30},{16,0},... | collective-permute-start | bytes 3870728 | tf_op jit(solution)/shard_map/ppermute | solution.py:151
  929.4 64.4 %collective-permute-start.46 = (f32[8,165888]{1,0:T(8,128)}, f32[8,165888]{1,0:T(8,128)}, u32[]{:S(2)}, u32[]{:S(2)}) collective-permute-start(f32[8,165888]{1,0:T(8,128)} %pad_maximum_fusion.4), channel_id=1, source_target_pairs={{0,2},{2,0},{4,6},{6,4},{8,10},{10,8},{12,14},{14,12},{16,18},{18,... | collective-permute-start | bytes 15925256 | tf_op jit(solution)/shard_map/ppermute | solution.py:122
  1064.8 45.9 %collective-permute-start.62 = (bf16[165888]{0:T(1024)(128)(2,1)S(1)}, bf16[165888]{0:T(1024)(128)(2,1)S(1)}, u32[]{:S(2)}, u32[]{:S(2)}) collective-permute-start(bf16[165888]{0:T(1024)(128)(2,1)S(1)} %convert_reduce_fusion.1), channel_id=1, source_target_pairs={{0,8},{2,10},{8,16},{10,18},{16,24},{18,26},{24,28},{26,30},{28,20... | collective-permute-start | bytes 995336 | tf_op jit(solution)/shard_map/ppermute | solution.py:132
  (166 other events, 3447.2 us)
